TPU v7x, 256 devices: a whole 4x4x8 slice. The times are simulated.
256 devices in a mesh: bucket: 64 (over x, y, z_hi), span: 4 (over z_lo, core).
Axes of the slice: x: 4, y: 4, z: 8 (z_hi: 4, z_lo: 2; z = z_hi * 2 + z_lo), core: 2. Of those that a mesh axis runs over, the one named last changes fastest.
Arguments:
- source_table: float32 [65536, 400], P('bucket'), may hold values from -6 to 6
- target_table: float32 [65536, 400], P('bucket'), may hold values from -6 to 6
- source_state: float32 [65536], P('bucket'), may hold values from 0.001 to 0.03
- target_state: float32 [65536], P('bucket'), may hold values from 0.001 to 0.03
- relation: float32 [16, 400], replicated, may hold values from -3 to 3
- relation_state: float32 [16], replicated, may hold values from 10 to 1000
- plan: int32 [64], replicated, may hold values from 0 to 63, each once
- source_index: int32 [64, 10240], P('bucket', 'span'), may hold values from 0 to 1023
- target_index: int32 [64, 10240], P('bucket', 'span'), may hold values from 0 to 1023
- relation_index: int32 [64, 10240], P('bucket', 'span'), may hold values from 0 to 15
- edge_counts: int32 [64], P('bucket'), may hold values from 1280 to 10240, as said below
Outputs:
- new_source: float32 [65536, 400], P('bucket')
- new_target: float32 [65536, 400], P('bucket')
- new_relation: float32 [16, 400], replicated
Inputs may be any that keep to these rules, and one draw needn't show every extreme that they name: `plan`: each partition index appears once. `edge_counts`: one bucket has exactly 10240 live slots and another exactly 1280.
All inputs are finite; a program needn't handle non-finite values.
Results may differ from a plain program's by a relative error of at most 0.0028.
The roundings to bfloat16 on the way count: a program that leaves them out, or rounds other values in their place, can miss the bound.
Values may be sent and summed in bfloat16 or wider, within the bound.
A program may use at most 64 MiB of HBM per device.

v0:
```python
import jax
import jax.numpy as jnp
from jax import lax
from jax.sharding import PartitionSpec as P

E_CH = 640


LEARN_RATE = 0.25
NEG_WEIGHT = 0.03125


def span_terms(head_rows, relation_rows, tail_rows, live_mask):
    half_width = head_rows.shape[1] // 2
    head_float = head_rows.astype(jnp.float32)
    head_real = head_float[:, :half_width]
    head_imag = head_float[:, half_width:]
    rel_real = relation_rows[:, :half_width]
    rel_imag = relation_rows[:, half_width:]
    query_rows = jnp.concatenate(
        [head_real * rel_real - head_imag * rel_imag, head_real * rel_imag + head_imag * rel_real],
        axis=1,
    ).astype(jnp.bfloat16)
    scores = lax.dot_general(
        query_rows, tail_rows, (((1,), (1,)), ((), ())), preferred_element_type=jnp.float32
    )
    diagonal = lax.broadcasted_iota(jnp.int32, scores.shape, 0) == lax.broadcasted_iota(
        jnp.int32, scores.shape, 1
    )
    weights = jnp.where(diagonal, -jax.nn.sigmoid(-scores), NEG_WEIGHT * jax.nn.sigmoid(scores))
    coefficients = (weights * live_mask[:, None] * live_mask[None, :]).astype(jnp.bfloat16)
    grad_query = jnp.dot(coefficients, tail_rows, preferred_element_type=jnp.float32)
    grad_tail = lax.dot_general(
        coefficients, query_rows, (((0,), (0,)), ((), ())), preferred_element_type=jnp.float32
    )
    query_real = grad_query[:, :half_width]
    query_imag = grad_query[:, half_width:]
    grad_head = jnp.concatenate(
        [
            query_real * rel_real + query_imag * rel_imag,
            query_imag * rel_real - query_real * rel_imag,
        ],
        axis=1,
    )
    grad_relation = jnp.concatenate(
        [
            query_real * head_real + query_imag * head_imag,
            query_imag * head_real - query_real * head_imag,
        ],
        axis=1,
    )
    return (grad_head, grad_relation, grad_tail)


def row_adagrad(weights, accumulated, gradient):
    summed = accumulated + jnp.mean(gradient * gradient, axis=1)
    return weights - LEARN_RATE * gradient / jnp.sqrt(summed)[:, None]


def route_blocks(row_block, selector):
    buckets = lax.axis_size("bucket")
    rows_total, feature_width = row_block.shape
    pieces = row_block.reshape(buckets, rows_total // buckets, feature_width)
    spread_out = lax.all_to_all(pieces, "bucket", split_axis=0, concat_axis=0, tiled=True)
    picker = (selector[:, None] == jnp.arange(buckets, dtype=jnp.int32)[None, :]).astype(
        jnp.float32
    )
    chosen = jnp.einsum("ij,jrd->ird", picker, spread_out, precision=lax.Precision.HIGHEST)
    arrived = lax.all_to_all(chosen, "bucket", split_axis=0, concat_axis=0, tiled=True)
    return arrived.reshape(rows_total, feature_width)


def per_device(
    source_table,
    target_table,
    source_state,
    target_state,
    relation,
    relation_state,
    plan,
    source_index,
    target_index,
    relation_index,
    edge_counts,
):
    num_buckets = lax.axis_size("bucket")
    lane_index = lax.axis_index("span")
    inverse = jnp.zeros_like(plan).at[plan].set(jnp.arange(num_buckets, dtype=jnp.int32))
    live_limit = edge_counts[0]
    table_rows, feature_width = source_table.shape
    spans_here = source_index.shape[1] // E_CH
    relation_count = relation.shape[0]
    relation_iota = jnp.arange(relation_count, dtype=jnp.int32)
    row_iota = jnp.arange(table_rows, dtype=jnp.int32)
    head_table = source_index.reshape(spans_here, E_CH)
    tail_table = target_index.reshape(spans_here, E_CH)
    kind_table = relation_index.reshape(spans_here, E_CH)
    starts = (lane_index * spans_here + jnp.arange(spans_here, dtype=jnp.int32)) * E_CH
    source_low = source_table.astype(jnp.bfloat16)
    target_low = route_blocks(target_table, plan).astype(jnp.bfloat16)

    def add_span(position_now, carried):
        span_start = starts[position_now]

        def compute(values):
            source_grad, target_grad, rel_grad = values
            slots = span_start + jnp.arange(E_CH, dtype=jnp.int32)
            live_mask = (slots < live_limit).astype(jnp.float32)
            head_ids = lax.dynamic_index_in_dim(head_table, position_now, 0, keepdims=False)
            tail_ids = lax.dynamic_index_in_dim(tail_table, position_now, 0, keepdims=False)
            kind_ids = lax.dynamic_index_in_dim(kind_table, position_now, 0, keepdims=False)
            one_hot = (kind_ids[:, None] == relation_iota[None, :]).astype(jnp.float32)
            relation_rows = jnp.dot(one_hot, relation, precision=lax.Precision.HIGHEST)
            head_match = head_ids[:, None] == row_iota[None, :]
            tail_match = tail_ids[:, None] == row_iota[None, :]
            head_rows = jnp.dot(
                head_match.astype(jnp.bfloat16), source_low, preferred_element_type=jnp.float32
            ).astype(jnp.bfloat16)
            tail_rows = jnp.dot(
                tail_match.astype(jnp.bfloat16), target_low, preferred_element_type=jnp.float32
            ).astype(jnp.bfloat16)
            grad_head, grad_relation, grad_tail = span_terms(
                head_rows, relation_rows, tail_rows, live_mask
            )
            rel_add = lax.dot_general(
                one_hot, grad_relation, (((0,), (0,)), ((), ())), precision=lax.Precision.HIGHEST
            )
            head_add = lax.dot_general(
                head_match.astype(jnp.float32),
                grad_head,
                (((0,), (0,)), ((), ())),
                precision=lax.Precision.HIGHEST,
            )
            tail_add = lax.dot_general(
                tail_match.astype(jnp.float32),
                grad_tail,
                (((0,), (0,)), ((), ())),
                precision=lax.Precision.HIGHEST,
            )
            return (source_grad + head_add, target_grad + tail_add, rel_grad + rel_add)

        def keep_values(values):
            return values

        return lax.cond(span_start < live_limit, compute, keep_values, carried)

    start_values = (
        jnp.zeros((table_rows, feature_width), jnp.float32),
        jnp.zeros((table_rows, feature_width), jnp.float32),
        jnp.zeros((relation_count, feature_width), jnp.float32),
    )
    source_grad, target_grad, rel_grad = lax.fori_loop(0, spans_here, add_span, start_values)
    rel_total = lax.psum(rel_grad, ("bucket", "span"))
    new_relation = row_adagrad(relation, relation_state, rel_total)
    source_sum, target_sum = lax.psum((source_grad, target_grad), "span")
    target_home = route_blocks(target_sum, inverse)
    new_source = row_adagrad(source_table, source_state, source_sum)
    new_target = row_adagrad(target_table, target_state, target_home)
    return (new_source, new_target, new_relation)


def solution(mesh):
    placed = (
        P("bucket", None),
        P("bucket", None),
        P("bucket"),
        P("bucket"),
        P(),
        P(),
        P(),
        P("bucket", "span"),
        P("bucket", "span"),
        P("bucket", "span"),
        P("bucket"),
    )
    return jax.shard_map(
        per_device,
        mesh=mesh,
        in_specs=placed,
        out_specs=(P("bucket", None), P("bucket", None), P()),
        check_vma=False,
    )
```

profile of v0, /device:TPU:1, one launch (start us, length us, event | category | flops | bytes accessed | tf_op | source)
XLA Modules:
  0.0 449.8 jit_solution(263234524063115752)
XLA Ops:
  7.2 1.8 copy.25
  9.0 66.5 %all_to_all.20 = f32[64,16,400]{2,1,0:T(8,128)S(1)} all-to-all(f32[64,16,400]{2,1,0:T(8,128)S(1)} %bitcast.26), channel_id=1, replica_groups=mesh['bucket'=64,'span'=4] {'bucket'}, dimensions={0} | all-to-all | bytes 3276800 | tf_op jit(solution)/shard_map/all_to_all | solution.py:64
  75.5 2.5 fusion.57
  78.0 1.5 copy.27
  79.6 6.5 %all-to-all-start.1 = ((bf16[64,16,400]{2,1,0:T(8,128)(2,1)}), bf16[64,16,400]{2,1,0:T(8,128)(2,1)S(1)}, u32[]{:S(2)}, u32[]{:S(2)}) async-start(bf16[64,16,400]{2,1,0:T(8,128)(2,1)} %copy.27), calls=%async_computation.1 | async-start | bytes 2097152 | tf_op jit(solution)/shard_map/all_to_all | solution.py:69
  86.5 1.4 copy.24
  87.9 21.9 %all-to-all-done.1 = bf16[64,16,400]{2,1,0:T(8,128)(2,1)S(1)} async-done(((bf16[64,16,400]{2,1,0:T(8,128)(2,1)}), bf16[64,16,400]{2,1,0:T(8,128)(2,1)S(1)}, u32[]{:S(2)}, u32[]{:S(2)}) %all-to-all-start.1) | async-done | bytes 819232 | tf_op jit(solution)/shard_map/all_to_all | solution.py:69
  109.7 1.0 copy-done.7
  111.5 63.1 %while.19 = (s32[]{:T(128)}, f32[1024,400]{0,1:T(8,128)S(1)}, f32[1024,400]{0,1:T(8,128)S(1)}, f32[16,400]{1,0:T(8,128)S(1)}, s32[4]{0:T(128)S(1)}, /*index=5*/s...) while((s32[]{:T(128)}, f32[1024,400]{0,1:T(8,128)S(1)}, ...), condition=%wide.region_3.4_spmd.clone.clone, body=%wide.region_0.3_spmd.clone.clone.sunk | while | flops 8435658752 | bytes 31468124 | solution.py:152
  113.3 13.9 %conditional.4 = ((f32[1024,400]{0,1:T(8,128)S(1)}, f32[1024,400]{0,1:T(8,128)S(1)}, f32[16,400]{1,0:T(8,128)S(1)})) conditional(s32[]{:T(128)} %convert_element_type.60, (f32[1024,400]{0,1:T(8,128)S(1)}, f32[1024,400]{0,1:T(8,128)S(1)}, f32[16,400]{1,0:T(8,128)S(1)}) %tuple.60, (s32[]{:T(128)}, s32[4,640]{1,0:T(4,128)S(1)}, s32[1024]{0:T(1024)S(1)}, ...), branch_computations={%region_1.1_spmd, %region_2.0_spmd} | conditional | flops 8435658752 | bytes 31463662 | solution.py:145
  113.4 2.3 fusion.32
  115.7 0.9 fusion.29
  116.7 1.3 fusion.49
  117.9 0.7 fusion.41
  118.8 0.9 multiply_convert_fusion
  120.4 0.7 fusion.67
  121.3 0.7 convolution_add_fusion
  122.1 2.6 fusion.15
  124.7 2.6 fusion.12
  129.1 13.9 %conditional.4 = ((f32[1024,400]{0,1:T(8,128)S(1)}, f32[1024,400]{0,1:T(8,128)S(1)}, f32[16,400]{1,0:T(8,128)S(1)})) conditional(s32[]{:T(128)} %convert_element_type.60, (f32[1024,400]{0,1:T(8,128)S(1)}, f32[1024,400]{0,1:T(8,128)S(1)}, f32[16,400]{1,0:T(8,128)S(1)}) %tuple.60, (s32[]{:T(128)}, s32[4,640]{1,0:T(4,128)S(1)}, s32[1024]{0:T(1024)S(1)}, ...), branch_computations={%region_1.1_spmd, %region_2.0_spmd} | conditional | flops 8435658752 | bytes 31463662 | solution.py:145
  129.2 2.3 fusion.32
  131.5 0.9 fusion.29
  132.4 1.3 fusion.49
  133.7 0.7 fusion.41
  134.6 0.9 multiply_convert_fusion
  135.5 0.7 fusion.43
  136.2 0.7 fusion.67
  137.1 0.7 convolution_add_fusion
  137.8 2.6 fusion.15
  140.4 2.6 fusion.12
  144.9 13.9 %conditional.4 = ((f32[1024,400]{0,1:T(8,128)S(1)}, f32[1024,400]{0,1:T(8,128)S(1)}, f32[16,400]{1,0:T(8,128)S(1)})) conditional(s32[]{:T(128)} %convert_element_type.60, (f32[1024,400]{0,1:T(8,128)S(1)}, f32[1024,400]{0,1:T(8,128)S(1)}, f32[16,400]{1,0:T(8,128)S(1)}) %tuple.60, (s32[]{:T(128)}, s32[4,640]{1,0:T(4,128)S(1)}, s32[1024]{0:T(1024)S(1)}, ...), branch_computations={%region_1.1_spmd, %region_2.0_spmd} | conditional | flops 8435658752 | bytes 31463662 | solution.py:145
  145.0 2.3 fusion.32
  147.3 0.9 fusion.29
  148.2 1.3 fusion.49
  149.5 0.7 fusion.41
  150.4 0.9 multiply_convert_fusion
  152.0 0.7 fusion.67
  152.9 0.7 convolution_add_fusion
  153.6 2.6 fusion.15
  156.2 2.6 fusion.12
  160.7 13.9 %conditional.4 = ((f32[1024,400]{0,1:T(8,128)S(1)}, f32[1024,400]{0,1:T(8,128)S(1)}, f32[16,400]{1,0:T(8,128)S(1)})) conditional(s32[]{:T(128)} %convert_element_type.60, (f32[1024,400]{0,1:T(8,128)S(1)}, f32[1024,400]{0,1:T(8,128)S(1)}, f32[16,400]{1,0:T(8,128)S(1)}) %tuple.60, (s32[]{:T(128)}, s32[4,640]{1,0:T(4,128)S(1)}, s32[1024]{0:T(1024)S(1)}, ...), branch_computations={%region_1.1_spmd, %region_2.0_spmd} | conditional | flops 8435658752 | bytes 31463662 | solution.py:145
  160.7 2.3 fusion.32
  163.0 0.9 fusion.29
  164.0 1.3 fusion.49
  165.3 0.7 fusion.41
  166.1 0.9 multiply_convert_fusion
  167.7 0.7 fusion.67
  168.7 0.7 convolution_add_fusion
  169.4 2.6 fusion.15
  172.0 2.6 fusion.12
  174.6 1.9 copy.28
  176.5 91.2 %all-reduce.3.cloned.1.call-done = (f32[1024,400]{0,1:T(8,128)}, f32[64,16,400]{2,1,0:T(8,128)}) async-done(((f32[1024,400]{0,1:T(8,128)}, f32[64,16,400]{2,1,0:T(8,128)}), (f32[1024,400]{0,1:T(8,128)}, f32[64,16,400]{2,1,0:T(8,128)})) %all-reduce.3.cloned.1.call-update) | async-done | bytes 3276816 | tf_op jit(solution)/shard_map/psum | solution.py:155
  267.7 11.7 %all-to-all-start.2 = ((f32[64,16,400]{2,1,0:T(8,128)}), f32[64,16,400]{2,1,0:T(8,128)S(1)}, u32[]{:S(2)}, u32[]{:S(2)}) async-start(f32[64,16,400]{2,1,0:T(8,128)} %get-tuple-element.395), calls=%async_computation.2 | async-start | bytes 4194304 | tf_op jit(solution)/shard_map/all_to_all | solution.py:64
  279.4 1.0 scatter_custom_fusion
  280.4 42.4 %all-to-all-done.2 = f32[64,16,400]{2,1,0:T(8,128)S(1)} async-done(((f32[64,16,400]{2,1,0:T(8,128)}), f32[64,16,400]{2,1,0:T(8,128)S(1)}, u32[]{:S(2)}, u32[]{:S(2)}) %all-to-all-start.2) | async-done | bytes 1638432 | tf_op jit(solution)/shard_map/all_to_all | solution.py:64
  322.8 2.5 fusion.55
  325.3 2.5 copy.30
  327.9 8.5 %all-to-all-start.3 = ((f32[64,16,400]{2,1,0:T(8,128)}), f32[64,16,400]{2,1,0:T(8,128)}, u32[]{:S(2)}, u32[]{:S(2)}) async-start(f32[64,16,400]{2,1,0:T(8,128)} %copy.30), calls=%async_computation.3 | async-start | bytes 4194304 | tf_op jit(solution)/shard_map/all_to_all | solution.py:69
  336.4 94.5 %psum.23 = f32[16,400]{1,0:T(8,128)S(1)} all-reduce(f32[16,400]{1,0:T(8,128)S(1)} %get-tuple-element.298), channel_id=1, replica_groups=mesh['bucket'=64,'span'=4] {'bucket','span'}, use_global_device_ids=true, to_apply=%region_9.10 | all-reduce | flops 6400 | bytes 51200 | tf_op jit(solution)/shard_map/psum | solution.py:153
  431.0 0.7 divide_subtract_fusion.1
  431.8 1.6 divide_subtract_fusion
  433.5 3.3 multiply_reduce_fusion
  437.0 3.2 fusion.54
  440.3 2.7 copy.34
  (92 shorter events, 7.7 us)
Async XLA Ops:
  9.0 66.5 %copy-start.1 = (f32[1024,400]{1,0:T(8,128)}, f32[1024,400]{1,0:T(8,128)S(1)}, u32[]{:S(2)}) copy-start(f32[1024,400]{1,0:T(8,128)S(1)} %copy.25) | copy-start | bytes 4915204
  9.0 66.5 %copy-start.14 = (s32[64]{0:T(128)S(1)}, s32[64]{0:T(128)}, u32[]{:S(2)}) copy-start(s32[64]{0:T(128)} %param.21) | copy-start | bytes 772
  78.0 8.3 %copy-start.9 = (s32[1,2560]{1,0:T(1,128)S(1)}, s32[1,2560]{1,0:T(1,128)}, u32[]{:S(2)}) copy-start(s32[1,2560]{1,0:T(1,128)} %param.22) | copy-start | bytes 30724
  78.0 8.4 %copy-start.10 = (s32[1,2560]{1,0:T(1,128)S(1)}, s32[1,2560]{1,0:T(1,128)}, u32[]{:S(2)}) copy-start(s32[1,2560]{1,0:T(1,128)} %param.23) | copy-start | bytes 30724
  78.0 8.4 %copy-start.11 = (s32[1,2560]{1,0:T(1,128)S(1)}, s32[1,2560]{1,0:T(1,128)}, u32[]{:S(2)}) copy-start(s32[1,2560]{1,0:T(1,128)} %param.24) | copy-start | bytes 30724
  79.6 6.9 %copy-start.4 = (f32[1024,400]{0,1:T(8,128)S(1)}, f32[1024,400]{0,1:T(8,128)}, u32[]{:S(2)}) copy-start(f32[1024,400]{0,1:T(8,128)} %param.15) | copy-start | bytes 4915204
  79.6 30.1 %all-to-all-start.1 = ((bf16[64,16,400]{2,1,0:T(8,128)(2,1)}), bf16[64,16,400]{2,1,0:T(8,128)(2,1)S(1)}, u32[]{:S(2)}, u32[]{:S(2)}) async-start(bf16[64,16,400]{2,1,0:T(8,128)(2,1)} %copy.27), calls=%async_computation.1 | async-start | bytes 2097152 | tf_op jit(solution)/shard_map/all_to_all | solution.py:69
  86.1 181.6 %all-reduce.3.cloned.1.call-start = ((), (), s32[]{:S(2)}) async-start(), calls=%async_computation.4 | async-start | bytes 7471104 | tf_op jit(solution)/shard_map/psum | solution.py:155
  109.7 1.0 copy-start.7
  110.7 0.8 copy-start.6
  113.4 2.3 copy-start.8
  129.2 2.3 copy-start.8
  144.9 2.3 copy-start.8
  160.7 2.3 copy-start.8
  174.5 1.9 copy-start
  267.7 55.2 %all-to-all-start.2 = ((f32[64,16,400]{2,1,0:T(8,128)}), f32[64,16,400]{2,1,0:T(8,128)S(1)}, u32[]{:S(2)}, u32[]{:S(2)}) async-start(f32[64,16,400]{2,1,0:T(8,128)} %get-tuple-element.395), calls=%async_computation.2 | async-start | bytes 4194304 | tf_op jit(solution)/shard_map/all_to_all | solution.py:64
  327.8 103.1 %copy-start.15 = (f32[16]{0:T(128)S(1)}, f32[16]{0:T(128)}, u32[]{:S(2)}) copy-start(f32[16]{0:T(128)} %param.20) | copy-start | bytes 196
  327.8 103.8 %copy-start.3 = (f32[1024,400]{0,1:T(8,128)S(1)}, f32[1024,400]{0,1:T(8,128)}, u32[]{:S(2)}) copy-start(f32[1024,400]{0,1:T(8,128)} %get-tuple-element.394) | copy-start | bytes 4915204
  327.9 105.6 %all-to-all-start.3 = ((f32[64,16,400]{2,1,0:T(8,128)}), f32[64,16,400]{2,1,0:T(8,128)}, u32[]{:S(2)}, u32[]{:S(2)}) async-start(f32[64,16,400]{2,1,0:T(8,128)} %copy.30), calls=%async_computation.3 | async-start | bytes 4194304 | tf_op jit(solution)/shard_map/all_to_all | solution.py:69
  336.3 95.5 %copy-start.12 = (f32[1024]{0:T(1024)S(1)}, f32[1024]{0:T(1024)}, u32[]{:S(2)}) copy-start(f32[1024]{0:T(1024)} %param.17) | copy-start | bytes 12292
  336.4 95.5 %copy-start.5 = (f32[1024,400]{0,1:T(8,128)S(1)}, f32[1024,400]{0,1:T(8,128)}, u32[]{:S(2)}) copy-start(f32[1024,400]{0,1:T(8,128)} %param.15) | copy-start | bytes 4915204
  433.5 3.5 copy-start.13
  433.5 3.5 copy-start.2
Sparse Core Ops, SparseCore 0:
  176.6 91.0 all-reduce.2
where the time goes:
time: 451 us; the launch traced here: 450 us
  blocking collectives  161 us (36%)
  waiting for transfers between devices  155 us (34%)
  matrix products  53.2 us (12%)
  starting transfers between devices  26.9 us (6%)
  local copies, waits for them, and re-layouts  17.6 us (4%)
  other arithmetic  15.7 us (3%)
  between operations  14.3 us (3%)
  loops' own time  5.71 us (1%)
    psum x1, blocking collectives, per_device(): rel_total = lax.psum(rel_grad, ('bucket', 'span'))  94.5 us
    psum x1, waiting for transfers between devices, per_device(): source_sum, target_sum = lax.psum((source_grad, target_grad), 'span')  91.2 us
    all_to_all x1, blocking collectives, route_blocks(): lax.all_to_all(pieces, 'bucket', split_axis=0, concat_axis=0, tiled=True)  66.5 us
    all_to_all x1, waiting for transfers between devices, route_blocks(): lax.all_to_all(pieces, 'bucket', split_axis=0, concat_axis=0, tiled=True)  42.4 us
    all_to_all x2, waiting for transfers between devices, route_blocks(): lax.all_to_all(chosen, 'bucket', split_axis=0, concat_axis=0, tiled=True)  21.9 us
    all_to_all x2, starting transfers between devices, route_blocks(): lax.all_to_all(chosen, 'bucket', split_axis=0, concat_axis=0, tiled=True)  15 us
    all_to_all x1, starting transfers between devices, route_blocks(): lax.all_to_all(pieces, 'bucket', split_axis=0, concat_axis=0, tiled=True)  11.7 us
    dot_general x4, matrix products, compute(): lax.dot_general(tail_match.astype(jnp.float32), grad_tail, (((0,), (0,)),...  10.3 us
  transfers between devices with their start and end apart: 4, of which 3 were waited for; matrix products, arithmetic and copies ran while one was open for 1% of the time, Pallas kernels for 0%

commit v1 on v0

v1 whole, which is shorter than its diff:
```python
import functools

import jax
import jax.numpy as jnp
from jax import lax
from jax.experimental import pallas as pl
from jax.experimental.pallas import tpu as pltpu
from jax.sharding import PartitionSpec as P

MESH = pl.DeviceIdType.MESH
BF = jnp.bfloat16
F32 = jnp.float32
E_CH = 640
LEARN_RATE = 0.25
NEG_WEIGHT = 0.03125
D = 400
HALF = 200
ROWS = 1024
Q = 256
EDGES = 2560
SPANS = 4
REL = 16
TILES = 50
CH = 5
CHROWS = D // CH
CHUNK = 512


class Place:
    def __init__(self):
        self.me = lax.axis_index("bucket")
        self.s = lax.axis_index("span")
        self.x = self.me // 16
        self.y = (self.me // 4) % 4
        self.z = self.me % 4
        self.buddy = self.s + 1 - 2 * (self.s % 2)
        self.cross = (self.s + 2) % 4
        self.diag = (self.buddy + 2) % 4

    def peer(self, k):
        return ((self.x + k // 16) % 4) * 16 + ((self.y + (k // 4) % 4) % 4) * 4 + (self.z + k % 4) % 4

    def slot(self, i):
        return (61 * i + 16 * self.s) % 64

    def greet(self):
        barrier = pltpu.get_barrier_semaphore()

        def sig(k, c):
            pl.semaphore_signal(barrier, inc=1, device_id=(self.peer(k), self.s), device_id_type=MESH)
            return c

        lax.fori_loop(1, 64, sig, 0)
        for o in (self.buddy, self.cross, self.diag):
            pl.semaphore_signal(barrier, inc=1, device_id=(self.me, o), device_id_type=MESH)
        return barrier


def tile_at(ref, j, lane0=0):
    return ref.at[
        pl.ds(pl.multiple_of(16 * (j // 2), 16), 16),
        pl.ds(pl.multiple_of(lane0 + 128 * (j % 2), 128), 128),
    ]


def wait_tiles(buf, n, ssem, rsem, pc, send):
    ref = buf.at[pl.ds(0, n)]
    d = pltpu.make_async_remote_copy(
        src_ref=ref, dst_ref=ref, send_sem=ssem, recv_sem=rsem, device_id=(pc.me, pc.buddy), device_id_type=MESH
    )
    if send:
        d.wait_send()
    else:
        d.wait_recv()


def leg_one(pc, src, recv, sem_loc, ssem, rsem):
    def go(k, c):
        p = pc.peer(k)
        j = pc.slot(p)

        @pl.when(j < TILES)
        def _():
            pltpu.make_async_remote_copy(
                src_ref=tile_at(src, j), dst_ref=recv.at[pc.me], send_sem=ssem, recv_sem=rsem,
                device_id=(p, pc.s), device_id_type=MESH,
            ).start()

        return c

    mine = pc.slot(pc.me)

    @pl.when(mine < TILES)
    def _():
        pltpu.make_async_copy(tile_at(src, mine), recv.at[pc.me], sem_loc).start()

    lax.fori_loop(1, 64, go, 0)


def leg_one_wait(pc, src, recv, sem_loc, ssem, rsem):
    mine = pc.slot(pc.me)

    @pl.when(mine < TILES)
    def _():
        pltpu.make_async_copy(tile_at(src, mine), recv.at[pc.me], sem_loc).wait()
        wait_tiles(recv, 63, ssem, rsem, pc, False)


def leg_two(pc, recv, pick, send, dst, sem_loc, ssem, rsem):
    mine = pc.slot(pc.me)
    lane0 = pc.s * Q

    @pl.when(mine < TILES)
    def _():
        for i in range(64):
            send[i] = recv[pick[i]]
        pltpu.make_async_copy(send.at[pc.me], tile_at(dst, mine, lane0), sem_loc).start()

        def go(k, c):
            p = pc.peer(k)
            pltpu.make_async_remote_copy(
                src_ref=send.at[p], dst_ref=tile_at(dst, mine, lane0), send_sem=ssem, recv_sem=rsem,
                device_id=(p, pc.s), device_id_type=MESH,
            ).start()
            return c

        lax.fori_loop(1, 64, go, 0)


def leg_two_wait(pc, recv, send, dst, sem_loc, ssem, rsem):
    mine = pc.slot(pc.me)

    @pl.when(mine < TILES)
    def _():
        pltpu.make_async_copy(send.at[pc.me], tile_at(dst, mine, pc.s * Q), sem_loc).wait()
        wait_tiles(recv, TILES - 1, ssem, rsem, pc, False)

    @pl.when(mine >= TILES)
    def _():
        wait_tiles(recv, TILES, ssem, rsem, pc, False)


def legs_sent(pc, recv, s1, s2, r1):
    mine = pc.slot(pc.me)

    @pl.when(mine < TILES)
    def _():
        wait_tiles(recv, TILES - 1, s1, r1, pc, True)
        wait_tiles(recv, 63, s2, r1, pc, True)

    @pl.when(mine >= TILES)
    def _():
        wait_tiles(recv, TILES, s1, r1, pc, True)


def lanes(q, n=Q):
    return pl.ds(pl.multiple_of(q * Q, Q), n)


def gather_quarters(pc, out, ssem, rsem):
    def cp(q, c, o, i):
        ref = out.at[pl.ds(c * CHROWS, CHROWS), lanes(q)]
        return pltpu.make_async_remote_copy(
            src_ref=ref, dst_ref=ref, send_sem=ssem.at[i, c], recv_sem=rsem.at[i, c],
            device_id=(pc.me, o), device_id_type=MESH,
        )

    across = [cp(pc.s, c, pc.cross, 0) for c in range(CH)]
    beside = [cp(pc.s, c, pc.buddy, 1) for c in range(CH)]
    passed = [cp(pc.cross, c, pc.buddy, 2) for c in range(CH)]
    for c in range(CH):
        across[c].start()
        beside[c].start()
    for c in range(CH):
        across[c].wait_recv()
        passed[c].start()
    for c in range(CH):
        beside[c].wait_recv()
        passed[c].wait_recv()
    for c in range(CH):
        across[c].wait_send()
        beside[c].wait_send()
        passed[c].wait_send()


def forward_kernel(tgt, plan, out, raw, send1, recv1, send2, sem_in, sem_loc, s1, r1, s2, r2, sag, rag):
    pc = Place()
    cin = pltpu.make_async_copy(tgt.at[:, lanes(pc.s)], raw, sem_in)
    cin.start()
    barrier = pc.greet()
    cin.wait()
    send1[...] = raw[...].astype(BF)
    pl.semaphore_wait(barrier, 66)
    leg_one(pc, send1, recv1, sem_loc, s1, r1)
    leg_one_wait(pc, send1, recv1, sem_loc, s1, r1)
    leg_two(pc, recv1, plan, send2, out, sem_loc, s2, r2)
    leg_two_wait(pc, recv1, send2, out, sem_loc, s2, r2)
    gather_quarters(pc, out, sag, rag)
    legs_sent(pc, recv1, s1, s2, r1)


def forward(target_t, plan):
    dma = pltpu.SemaphoreType.DMA
    return pl.pallas_call(
        forward_kernel,
        out_shape=jax.ShapeDtypeStruct((D, ROWS), BF),
        in_specs=[pl.BlockSpec(memory_space=pl.ANY), pl.BlockSpec(memory_space=pltpu.SMEM)],
        out_specs=pl.BlockSpec(memory_space=pltpu.VMEM),
        scratch_shapes=[
            pltpu.VMEM((D, Q), F32), pltpu.VMEM((D, Q), BF),
            pltpu.VMEM((64, 16, 128), BF), pltpu.VMEM((64, 16, 128), BF),
            dma, dma, dma, dma, dma, dma, dma((3, CH)), dma((3, CH)),
        ],
        compiler_params=pltpu.CompilerParams(collective_id=0, has_side_effects=True, vmem_limit_bytes=24 << 20),
        name="forward_route",
    )(target_t, plan)


def dot(a, b, ca=1, cb=0):
    return lax.dot_general(a, b, (((ca,), (cb,)), ((), ())), preferred_element_type=F32)


def spans_kernel(src, tgt, rel, sidx, tidx, kidx, lim, plan, o_src, o_tgt, o_rel, o_inv,
                 low, heads, tails, kinds, query, head, tail, relrow, coef, gtail, ghead, grel):
    first = lax.axis_index("span") * EDGES
    for b in range(64):
        o_inv[plan[b]] = b
    low[...] = src[...].astype(BF)
    r = rel[...]
    hi = r.astype(BF)
    mid = (r - hi.astype(F32)).astype(BF)
    lo = (r - hi.astype(F32) - mid.astype(F32)).astype(BF)
    rel3 = jnp.concatenate([hi, mid, lo], axis=0)

    def gather(c, carry):
        at = pl.ds(pl.multiple_of(c * CHUNK, CHUNK), CHUNK)
        slots = first + c * CHUNK + lax.broadcasted_iota(jnp.int32, (1, CHUNK), 1)
        alive = slots < lim[0]
        rows = lax.broadcasted_iota(jnp.int32, (ROWS, CHUNK), 0)
        hot = (rows == jnp.where(alive, sidx[:, at], -1)).astype(F32).astype(BF)
        heads[:, at] = hot
        h = dot(low[...], hot)
        head[:, at] = h.astype(BF)
        kind = jnp.where(alive, kidx[:, at], -1)
        k16 = lax.broadcasted_iota(jnp.int32, (REL, CHUNK), 0)
        khot = (k16 == kind).astype(F32).astype(BF)
        kinds[:, at] = khot
        rr = dot(rel3, jnp.concatenate([khot, khot, khot], axis=0), 0, 0)
        relrow[:, at] = rr
        hr, hm, rr_, rm = h[:HALF], h[HALF:], rr[:HALF], rr[HALF:]
        query[:, at] = jnp.concatenate([hr * rr_ - hm * rm, hr * rm + hm * rr_], axis=0).astype(BF)
        hot = (rows == jnp.where(alive, tidx[:, at], -1)).astype(F32).astype(BF)
        tails[:, at] = hot
        tail[:, at] = dot(tgt[...], hot).astype(BF)
        return carry

    lax.fori_loop(0, EDGES // CHUNK, gather, 0)

    def span(k, carry):
        base = pl.multiple_of(k * E_CH, 128)
        at = pl.ds(base, E_CH)
        for b in range(E_CH // 128):
            qb = query[:, pl.ds(pl.multiple_of(base + 128 * b, 128), 128)]
            score = dot(qb, tail[:, at], 0, 0)
            for j in range(E_CH // 128):
                u = score[:, 128 * j:128 * j + 128]
                if j == b:
                    diag = lax.broadcasted_iota(jnp.int32, (128, 128), 0) == lax.broadcasted_iota(jnp.int32, (128, 128), 1)
                    w = jax.nn.sigmoid(jnp.where(diag, -u, u)) * jnp.where(diag, -1.0, NEG_WEIGHT)
                else:
                    w = jax.nn.sigmoid(u) * NEG_WEIGHT
                coef[pl.ds(128 * b, 128), pl.ds(128 * j, 128)] = w.astype(BF)
        gtail[:, at] = dot(query[:, at], coef[...]).astype(BF)
        gq = dot(tail[:, at], coef[...], 1, 1)
        gr, gm = gq[:HALF], gq[HALF:]
        rr = relrow[:, at]
        rr_, rm = rr[:HALF], rr[HALF:]
        h = head[:, at].astype(F32)
        hr, hm = h[:HALF], h[HALF:]
        ghead[:, at] = jnp.concatenate([gr * rr_ + gm * rm, gm * rr_ - gr * rm], axis=0).astype(BF)
        grel[:, at] = jnp.concatenate([gr * hr + gm * hm, gm * hr - gr * hm], axis=0).astype(BF)
        return carry

    lax.fori_loop(0, SPANS, span, 0)
    o_tgt[...] = dot(gtail[...], tails[...], 1, 1).astype(BF)
    o_src[...] = dot(ghead[...], heads[...], 1, 1).astype(BF)
    o_rel[:, 0:D] = dot(kinds[...], grel[...], 1, 1)
    o_rel[:, D:512] = jnp.zeros((REL, 512 - D), F32)


def spans(source_t, target_low, relation, sidx, tidx, kidx, counts, plan):
    vm = pl.BlockSpec(memory_space=pltpu.VMEM)
    sm = pl.BlockSpec(memory_space=pltpu.SMEM)
    return pl.pallas_call(
        spans_kernel,
        out_shape=(
            jax.ShapeDtypeStruct((D, ROWS), BF), jax.ShapeDtypeStruct((D, ROWS), BF),
            jax.ShapeDtypeStruct((REL, 512), F32), jax.ShapeDtypeStruct((64,), jnp.int32),
        ),
        in_specs=[vm, vm, vm, vm, vm, vm, sm, sm],
        out_specs=(vm, vm, vm, sm),
        scratch_shapes=[
            pltpu.VMEM((D, ROWS), BF), pltpu.VMEM((ROWS, EDGES), BF), pltpu.VMEM((ROWS, EDGES), BF), pltpu.VMEM((REL, EDGES), BF),
            pltpu.VMEM((D, EDGES), BF), pltpu.VMEM((D, EDGES), BF), pltpu.VMEM((D, EDGES), BF), pltpu.VMEM((D, EDGES), F32),
            pltpu.VMEM((E_CH, E_CH), BF), pltpu.VMEM((D, EDGES), BF), pltpu.VMEM((D, EDGES), BF), pltpu.VMEM((D, EDGES), BF),
        ],
        compiler_params=pltpu.CompilerParams(vmem_limit_bytes=50 << 20),
        name="spans",
    )(source_t, target_low, relation, sidx, tidx, kidx, counts, plan)


def back_kernel(sg, tg, rg, inv, o_src, o_tgt, o_rel,
                t1, t2send, t2, quarter, recv1, send2, half, halfin, halfx, r1buf, r2buf, r2send, rax, sem_loc, st, rt,
                s1, rc1, s2, rc2, sag, rag, srel, rrel):
    pc = Place()
    barrier = pc.greet()
    pl.semaphore_wait(barrier, 66)

    def rc(src, dst, i, o):
        return pltpu.make_async_remote_copy(
            src_ref=src, dst_ref=dst, send_sem=st.at[i], recv_sem=rt.at[i], device_id=(pc.me, o), device_id_type=MESH
        )

    def to_bucket(src, dst, i, p):
        return pltpu.make_async_remote_copy(
            src_ref=src, dst_ref=dst, send_sem=srel.at[i], recv_sem=rrel.at[i], device_id=(p, pc.s), device_id_type=MESH
        )

    ta = rc(tg.at[:, lanes(pc.diag)], t1.at[1], 0, pc.buddy)
    tb = rc(tg.at[:, lanes(pc.buddy)], t1.at[0], 1, pc.buddy)
    sa = rc(sg.at[:, lanes(pc.buddy)], halfin.at[0], 2, pc.buddy)
    sb = rc(sg.at[:, lanes(pc.diag)], halfin.at[1], 3, pc.buddy)
    ra = rc(rg, r1buf, 4, pc.buddy)
    for c in (ta, tb, ra, sa, sb):
        c.start()
    ta.wait_recv()
    t2send[...] = (tg[:, lanes(pc.cross)].astype(F32) + t1[1].astype(F32)).astype(BF)
    tc = rc(t2send, t2, 5, pc.cross)
    tc.start()
    ra.wait_recv()
    r2send[...] = rg[...] + r1buf[...]
    rb = rc(r2send, r2buf, 6, pc.cross)
    rb.start()
    sa.wait_recv()
    half[0] = (sg[:, lanes(pc.s)].astype(F32) + halfin[0].astype(F32)).astype(BF)
    sb.wait_recv()
    half[1] = (sg[:, lanes(pc.cross)].astype(F32) + halfin[1].astype(F32)).astype(BF)
    tb.wait_recv()
    tc.wait_recv()
    quarter[...] = (tg[:, lanes(pc.s)].astype(F32) + t1[0].astype(F32) + t2[...].astype(F32)).astype(BF)
    leg_one(pc, quarter, recv1, sem_loc, s1, rc1)
    rb.wait_recv()
    col = pl.ds(pl.multiple_of(pc.s * 128, 128), 128)
    px = [((pc.x + d) % 4) * 16 + pc.y * 4 + pc.z for d in (1, 2, 3)]
    py = [pc.x * 16 + ((pc.y + d) % 4) * 4 + pc.z for d in (1, 2, 3)]
    pz = [pc.x * 16 + pc.y * 4 + (pc.z + d) % 4 for d in (1, 2, 3)]

    def axis(i, coord, peers, total):
        rax[i, coord] = total
        for p in peers:
            to_bucket(rax.at[i, coord], rax.at[i, coord], i, p).start()

    def axis_wait(i, send=False):
        ref = rax.at[i, pl.ds(0, 3)]
        d = to_bucket(ref, ref, i, px[0])
        if send:
            d.wait_send()
            return None
        d.wait_recv()
        return (rax[i, 0] + rax[i, 1]) + (rax[i, 2] + rax[i, 3])

    axis(0, pc.x, px, r2send[:, col] + r2buf[:, col])
    leg_one_wait(pc, quarter, recv1, sem_loc, s1, rc1)
    leg_two(pc, recv1, inv, send2, o_tgt, sem_loc, s2, rc2)
    sc = rc(half.at[0], halfx.at[1], 7, pc.cross)
    sd = rc(half.at[1], halfx.at[0], 8, pc.cross)
    sc.start()
    sd.start()
    axis(1, pc.y, py, axis_wait(0))
    axis(2, pc.z, pz, axis_wait(1))
    sc.wait_recv()
    sd.wait_recv()
    o_src[:, lanes(pc.s)] = (half[0].astype(F32) + halfx[0].astype(F32)).astype(BF)
    o_src[:, lanes(pc.cross)] = (half[1].astype(F32) + halfx[1].astype(F32)).astype(BF)
    se = rc(o_src.at[:, lanes(pc.s)], o_src.at[:, lanes(pc.s)], 9, pc.buddy)
    sf = rc(o_src.at[:, lanes(pc.cross)], o_src.at[:, lanes(pc.cross)], 10, pc.buddy)
    se.start()
    sf.start()
    o_rel[:, col] = axis_wait(2)
    rel_out = [rc(o_rel.at[:, col], o_rel.at[:, col], 11 + i, o) for i, o in enumerate((pc.buddy, pc.cross, pc.diag))]
    for c in rel_out:
        c.start()
    leg_two_wait(pc, recv1, send2, o_tgt, sem_loc, s2, rc2)
    gather_quarters(pc, o_tgt, sag, rag)
    for c in (se, sf, *rel_out):
        c.wait_recv()
    for c in (ta, tb, tc, sa, sb, sc, sd, se, sf, ra, rb, *rel_out):
        c.wait_send()
    for i in range(3):
        axis_wait(i, True)
    legs_sent(pc, recv1, s1, s2, rc1)


def back(sg, tg, rg, inv):
    vm = pl.BlockSpec(memory_space=pltpu.VMEM)
    dma = pltpu.SemaphoreType.DMA
    two = pltpu.VMEM((2, D, Q), BF)
    one = pltpu.VMEM((D, Q), BF)
    big = pltpu.VMEM((REL, 512), F32)
    return pl.pallas_call(
        back_kernel,
        out_shape=(
            jax.ShapeDtypeStruct((D, ROWS), BF), jax.ShapeDtypeStruct((D, ROWS), BF), jax.ShapeDtypeStruct((REL, 512), F32),
        ),
        in_specs=[vm, vm, vm, pl.BlockSpec(memory_space=pltpu.SMEM)],
        out_specs=(vm, vm, vm),
        scratch_shapes=[
            two, one, one, one, pltpu.VMEM((64, 16, 128), BF), pltpu.VMEM((64, 16, 128), BF), two, two, two,
            big, big, big, pltpu.VMEM((3, 4, REL, 128), F32),
            dma, dma((14,)), dma((14,)), dma, dma, dma, dma, dma((3, CH)), dma((3, CH)), dma((3,)), dma((3,)),
        ],
        compiler_params=pltpu.CompilerParams(collective_id=1, has_side_effects=True, vmem_limit_bytes=32 << 20),
        name="back_route",
    )(sg, tg, rg, inv)


def adagrad_kernel(ws, ss, gs, wt, st, gt, wr, sr, gr, o_s, o_t, o_r):
    for w, s, g, o in ((ws, ss, gs, o_s), (wt, st, gt, o_t)):
        grad = g[...].astype(F32)
        total = s[...] + jnp.sum(grad * grad, axis=0, keepdims=True) * (1.0 / D)
        o[...] = w[...] - (LEARN_RATE * grad) / jnp.sqrt(total)

    @pl.when(pl.program_id(0) == 0)
    def _():
        grad = gr[:, 0:D]
        total = sr[...] + jnp.sum(grad * grad, axis=1, keepdims=True) * (1.0 / D)
        o_r[...] = wr[...] - (LEARN_RATE * grad) / jnp.sqrt(total)


def adagrad(ws, ss, gs, wt, st, gt, wr, sr, gr):
    n = 256
    tab = pl.BlockSpec((D, n), lambda i: (0, i))
    row = pl.BlockSpec((1, n), lambda i: (0, i))
    whole = lambda *s: pl.BlockSpec(s, lambda i: (0,) * len(s))
    return pl.pallas_call(
        adagrad_kernel,
        grid=(ROWS // n,),
        out_shape=(
            jax.ShapeDtypeStruct((D, ROWS), F32), jax.ShapeDtypeStruct((D, ROWS), F32), jax.ShapeDtypeStruct((REL, D), F32),
        ),
        in_specs=[tab, row, tab, tab, row, tab, whole(REL, D), whole(REL, 1), whole(REL, 512)],
        out_specs=(tab, tab, whole(REL, D)),
        compiler_params=pltpu.CompilerParams(vmem_limit_bytes=24 << 20),
        name="adagrad",
    )(ws, ss, gs, wt, st, gt, wr, sr, gr)


def per_device(source_table, target_table, source_state, target_state, relation, relation_state,
               plan, source_index, target_index, relation_index, edge_counts):
    source_t, target_t = source_table.T, target_table.T
    target_low = forward(target_t, plan)
    sg, tg, rg, inv = spans(source_t, target_low, relation, source_index, target_index, relation_index, edge_counts, plan)
    sg, tg, rg = back(sg, tg, rg, inv)
    ns, nt, nr = adagrad(
        source_t, source_state[None, :], sg, target_t, target_state[None, :], tg, relation, relation_state[:, None], rg
    )
    return ns.T, nt.T, nr


def solution(mesh):
    placed = (
        P("bucket", None), P("bucket", None), P("bucket"), P("bucket"), P(), P(), P(),
        P("bucket", "span"), P("bucket", "span"), P("bucket", "span"), P("bucket"),
    )
    return jax.shard_map(
        per_device,
        mesh=mesh,
        in_specs=placed,
        out_specs=(P("bucket", None), P("bucket", None), P()),
        check_vma=False,
    )
```

time: 451 us -> 117 us (0.26)
  blocking collectives: 161 us -> 0 us
  waiting for transfers between devices: 155 us -> 0 us
  Pallas kernels: 0 us -> 113 us
  matrix products: 53.2 us -> 0 us
  starting transfers between devices: 26.9 us -> 0 us
  other arithmetic: 15.7 us -> 0 us
  local copies, waits for them, and re-layouts: 17.6 us -> 2.86 us
  between operations: 14.3 us -> 1.42 us
  loops' own time: 5.71 us -> 0 us
    pallas_call x0 -> x4, Pallas kernels: none -> 113 us  [the longest x1 48.7 us: back(): pl.pallas_call(back_kernel, out_shape=(jax.ShapeDtypeStruct((D, ROWS), BF...]
    psum x1 -> x0, blocking collectives: 94.5 us -> none  [per_device(): rel_total = lax.psum(rel_grad, ('bucket', 'span'))]
    psum x1 -> x0, waiting for transfers between devices: 91.2 us -> none  [per_device(): source_sum, target_sum = lax.psum((source_grad, target_grad), 'span')]
    all_to_all x1 -> x0, blocking collectives: 66.5 us -> none  [route_blocks(): lax.all_to_all(pieces, 'bucket', split_axis=0, concat_axis=0, tiled=True)]
    all_to_all x3 -> x0, waiting for transfers between devices: 64.3 us -> none  [the longest x1 42.4 us: route_blocks(): lax.all_to_all(pieces, 'bucket', split_axis=0, concat_axis=0, tiled=True)]
    dot_general x38 -> x0, matrix products: 53.2 us -> none  [the longest x4 10.3 us: compute(): lax.dot_general(tail_match.astype(jnp.float32), grad_tail, (((0,), (0,)),...]
    all_to_all x3 -> x0, starting transfers between devices: 26.7 us -> none  [the longest x2 15 us: route_blocks(): lax.all_to_all(chosen, 'bucket', split_axis=0, concat_axis=0, tiled=True)]
    another operation x5 -> x0, loops' own time: 5.71 us -> none  [the longest x1 5.23 us: per_device(): lax.fori_loop(0, spans_here, add_span, start_values)]
  transfers between devices with their start and end apart: 4 -> 0, of which waited for: 3 -> 0; matrix products, arithmetic and copies ran while one was open for 1% -> 0% of each run, Pallas kernels for 0% -> 0%
where the time goes in v1:
time: 117 us
  Pallas kernels  113 us (97%)
  local copies, waits for them, and re-layouts  2.86 us (2%)
  between operations  1.42 us (1%)
    pallas_call x1, Pallas kernels, back(): pl.pallas_call(back_kernel, out_shape=(jax.ShapeDtypeStruct((D, ROWS), BF...  48.7 us
    pallas_call x1, Pallas kernels, forward(): pl.pallas_call(forward_kernel, out_shape=jax.ShapeDtypeStruct((D, ROWS),...  39.7 us
    pallas_call x1, Pallas kernels, spans(): pl.pallas_call(spans_kernel, out_shape=(jax.ShapeDtypeStruct((D, ROWS), B...  21.1 us
    pallas_call x1, Pallas kernels, adagrad(): pl.pallas_call(adagrad_kernel, grid=(ROWS // n,), out_shape=(jax.ShapeDty...  3.03 us

profile of v1, /device:TPU:1, one launch (start us, length us, event | category | flops | bytes accessed | tf_op | source)
XLA Modules:
  0.0 116.8 jit_solution(1343155707558287763)
XLA Ops:
  0.6 0.0 copy-start.4
  1.3 0.7 copy.14.sr
  2.0 0.0 copy-start.1
  2.0 1.4 %copy-done.1 = f32[1024,400]{0,1:T(8,128)S(1)} copy-done((f32[1024,400]{0,1:T(8,128)S(1)}, f32[1024,400]{0,1:T(8,128)}, u32[]{:S(2)}) %copy-start.1) | copy-done | bytes 1638424
  3.5 0.0 copy-start.9
  3.5 0.7 copy-done.9
  4.1 0.0 copy-start.3
  4.1 0.0 copy-start.5
  4.1 0.0 copy-start.6
  4.1 39.7 %forward_route.1.tgt = bf16[400,1024]{1,0:T(8,128)(2,1)S(1)} custom-call(f32[400,1024]{1,0:T(8,128)S(1)} %bitcast.9, s32[64]{0:T(128)S(1)} %copy-done.9), custom_call_target="tpu_custom_call" | custom-call | tf_op jit(solution)/shard_map/forward_route/pallas_call | solution.py:204
  43.9 0.0 copy-done.4
  43.9 0.0 copy-done.3
  43.9 0.0 copy-done.5
  43.9 0.0 copy-done.6
  43.9 0.0 copy-start
  43.9 0.0 copy-start.2
  43.9 0.0 copy-start.7
  43.9 0.0 copy-start.8
  44.0 21.1 %spans.1 = (bf16[400,1024]{1,0:T(8,128)(2,1)S(1)}, bf16[400,1024]{1,0:T(8,128)(2,1)S(1)}, f32[16,512]{1,0:T(8,128)S(1)}, s32[64]{0:T(128)S(1)}) custom-call(f32[400,1024]{1,0:T(8,128)} %bitcast.7, bf16[400,1024]{1,0:T(8,128)(2,1)S(1)} %forward_route.1.tgt, f32[16,400]{1,0:T(8,128)S(1)} %copy-done.3, s32[1,2560]{1,0:T(1,128)S(1)} %copy-done.4, ...), custom_call_target="tpu_custom_call" | custom-call | tf_op jit(solution)/shard_map/spans/pallas_call | solution.py:294
  65.0 48.7 %back_route.1 = (bf16[400,1024]{1,0:T(8,128)(2,1)S(1)}, bf16[400,1024]{1,0:T(8,128)(2,1)S(1)}, f32[16,512]{1,0:T(8,128)S(1)}) custom-call(bf16[400,1024]{1,0:T(8,128)(2,1)S(1)} %get-tuple-element.13.sg, bf16[400,1024]{1,0:T(8,128)(2,1)S(1)} %get-tuple-element.14.tg, f32[16,512]{1,0:T(8,128)S(1)} %get-tuple-element.15.rg, s32[64]{0:T(128)S(1)} %get-tuple-element.16.inv), custom_call_target="tpu_custom_call" | custom-call | tf_op jit(solution)/shard_map/back_route/pallas_call | solution.py:410
  113.7 0.0 copy-done
  113.7 0.0 copy-done.2
  113.7 0.0 copy-done.7
  113.8 0.0 copy-done.8
  113.8 3.0 %adagrad.1 = (f32[400,1024]{1,0:T(8,128)}, f32[400,1024]{1,0:T(8,128)}, f32[16,400]{1,0:T(8,128)}) custom-call(f32[400,1024]{1,0:T(8,128)S(1)} %bitcast.8, f32[1,1024]{1,0:T(1,128)S(1)} %bitcast.11, bf16[400,1024]{1,0:T(8,128)(2,1)S(1)} %get-tuple-element.17.gs, f32[400,1024]{1,0:T(8,128)S(1)} %bitcast.10, f32[1,1024]{1,0:T(1,128)S(1)} %bitcast.12, ...), custom_call_target="tpu_custom_call" | custom-call | tf_op jit(solution)/shard_map/adagrad/pallas_call | solution.py:445
Async XLA Ops:
  0.6 43.2 %copy-start.4 = (s32[1,2560]{1,0:T(1,128)S(1)}, s32[1,2560]{1,0:T(1,128)}, u32[]{:S(2)}) copy-start(s32[1,2560]{1,0:T(1,128)} %sidx.1) | copy-start | bytes 30724
  2.0 1.4 %copy-start.1 = (f32[1024,400]{0,1:T(8,128)S(1)}, f32[1024,400]{0,1:T(8,128)}, u32[]{:S(2)}) copy-start(f32[1024,400]{0,1:T(8,128)} %param.12) | copy-start | bytes 4915204
  3.5 0.7 copy-start.9
  4.1 39.8 %copy-start.3 = (f32[16,400]{1,0:T(8,128)S(1)}, f32[16,400]{1,0:T(8,128)}, u32[]{:S(2)}) copy-start(f32[16,400]{1,0:T(8,128)} %wr.1) | copy-start | bytes 76804
  4.1 39.8 %copy-start.5 = (s32[1,2560]{1,0:T(1,128)S(1)}, s32[1,2560]{1,0:T(1,128)}, u32[]{:S(2)}) copy-start(s32[1,2560]{1,0:T(1,128)} %tidx.1) | copy-start | bytes 30724
  4.1 39.8 %copy-start.6 = (s32[1,2560]{1,0:T(1,128)S(1)}, s32[1,2560]{1,0:T(1,128)}, u32[]{:S(2)}) copy-start(s32[1,2560]{1,0:T(1,128)} %kidx.1) | copy-start | bytes 30724
  43.9 69.8 %copy-start = (f32[1024,400]{0,1:T(8,128)S(1)}, f32[1024,400]{0,1:T(8,128)}, u32[]{:S(2)}) copy-start(f32[1024,400]{0,1:T(8,128)} %param.11) | copy-start | bytes 4915204
  43.9 69.8 %copy-start.2 = (f32[1024,400]{0,1:T(8,128)S(1)}, f32[1024,400]{0,1:T(8,128)}, u32[]{:S(2)}) copy-start(f32[1024,400]{0,1:T(8,128)} %param.12) | copy-start | bytes 4915204
  43.9 69.8 %copy-start.7 = (f32[1024]{0:T(1024)S(1)}, f32[1024]{0:T(1024)}, u32[]{:S(2)}) copy-start(f32[1024]{0:T(1024)} %param.13) | copy-start | bytes 12292
  43.9 69.8 %copy-start.8 = (f32[1024]{0:T(1024)S(1)}, f32[1024]{0:T(1024)}, u32[]{:S(2)}) copy-start(f32[1024]{0:T(1024)} %param.14) | copy-start | bytes 12292

commit v2 on v1

v2 whole, which is shorter than its diff:
```python
import functools

import jax
import jax.numpy as jnp
from jax import lax
from jax.experimental import pallas as pl
from jax.experimental.pallas import tpu as pltpu
from jax.sharding import PartitionSpec as P

MESH = pl.DeviceIdType.MESH
BF = jnp.bfloat16
F32 = jnp.float32
E_CH = 640
LEARN_RATE = 0.25
NEG_WEIGHT = 0.03125
D = 400
HALF = 200
ROWS = 1024
Q = 256
EDGES = 2560
SPANS = 4
REL = 16
TILES = 50
CH = 5
CHROWS = D // CH
CHUNK = 512


class Place:
    def __init__(self):
        self.me = lax.axis_index("bucket")
        self.s = lax.axis_index("span")
        self.x = self.me // 16
        self.y = (self.me // 4) % 4
        self.z = self.me % 4
        self.buddy = self.s + 1 - 2 * (self.s % 2)
        self.cross = (self.s + 2) % 4
        self.diag = (self.buddy + 2) % 4

    def peer(self, k):
        return ((self.x + k // 16) % 4) * 16 + ((self.y + (k // 4) % 4) % 4) * 4 + (self.z + k % 4) % 4

    def slot(self, i):
        return (61 * i + 16 * self.s) % 64

    def greet(self):
        barrier = pltpu.get_barrier_semaphore()

        def sig(k, c):
            pl.semaphore_signal(barrier, inc=1, device_id=(self.peer(k), self.s), device_id_type=MESH)
            return c

        lax.fori_loop(1, 64, sig, 0)
        for o in (self.buddy, self.cross, self.diag):
            pl.semaphore_signal(barrier, inc=1, device_id=(self.me, o), device_id_type=MESH)
        return barrier


def tile_at(ref, j, lane0=0):
    return ref.at[
        pl.ds(pl.multiple_of(16 * (j // 2), 16), 16),
        pl.ds(pl.multiple_of(lane0 + 128 * (j % 2), 128), 128),
    ]


def wait_tiles(buf, n, ssem, rsem, pc, send):
    ref = buf.at[pl.ds(0, n)]
    d = pltpu.make_async_remote_copy(
        src_ref=ref, dst_ref=ref, send_sem=ssem, recv_sem=rsem, device_id=(pc.me, pc.buddy), device_id_type=MESH
    )
    if send:
        d.wait_send()
    else:
        d.wait_recv()


def leg_one(pc, src, recv, sem_loc, ssem, rsem):
    def go(k, c):
        p = pc.peer(k)
        j = pc.slot(p)

        @pl.when(j < TILES)
        def _():
            pltpu.make_async_remote_copy(
                src_ref=tile_at(src, j), dst_ref=recv.at[pc.me], send_sem=ssem, recv_sem=rsem,
                device_id=(p, pc.s), device_id_type=MESH,
            ).start()

        return c

    mine = pc.slot(pc.me)

    @pl.when(mine < TILES)
    def _():
        pltpu.make_async_copy(tile_at(src, mine), recv.at[pc.me], sem_loc).start()

    lax.fori_loop(1, 64, go, 0)


def leg_one_wait(pc, src, recv, sem_loc, ssem, rsem):
    mine = pc.slot(pc.me)

    @pl.when(mine < TILES)
    def _():
        pltpu.make_async_copy(tile_at(src, mine), recv.at[pc.me], sem_loc).wait()
        wait_tiles(recv, 63, ssem, rsem, pc, False)


def leg_two(pc, recv, pick, send, dst, sem_loc, ssem, rsem):
    mine = pc.slot(pc.me)
    lane0 = pc.s * Q

    @pl.when(mine < TILES)
    def _():
        for i in range(64):
            send[i] = recv[pick[i]]
        pltpu.make_async_copy(send.at[pc.me], tile_at(dst, mine, lane0), sem_loc).start()

        def go(k, c):
            p = pc.peer(k)
            pltpu.make_async_remote_copy(
                src_ref=send.at[p], dst_ref=tile_at(dst, mine, lane0), send_sem=ssem, recv_sem=rsem,
                device_id=(p, pc.s), device_id_type=MESH,
            ).start()
            return c

        lax.fori_loop(1, 64, go, 0)


def leg_two_wait(pc, recv, send, dst, sem_loc, ssem, rsem):
    mine = pc.slot(pc.me)

    @pl.when(mine < TILES)
    def _():
        pltpu.make_async_copy(send.at[pc.me], tile_at(dst, mine, pc.s * Q), sem_loc).wait()
        wait_tiles(recv, TILES - 1, ssem, rsem, pc, False)

    @pl.when(mine >= TILES)
    def _():
        wait_tiles(recv, TILES, ssem, rsem, pc, False)


def legs_sent(pc, recv, s1, s2, r1):
    mine = pc.slot(pc.me)

    @pl.when(mine < TILES)
    def _():
        wait_tiles(recv, TILES - 1, s1, r1, pc, True)
        wait_tiles(recv, 63, s2, r1, pc, True)

    @pl.when(mine >= TILES)
    def _():
        wait_tiles(recv, TILES, s1, r1, pc, True)


def lanes(q, n=Q):
    return pl.ds(pl.multiple_of(q * Q, Q), n)


def dot(a, b, ca=1, cb=0):
    return lax.dot_general(a, b, (((ca,), (cb,)), ((), ())), preferred_element_type=F32)


def quarter_rows(q):
    return pl.ds(pl.multiple_of(q * Q, Q), Q)


def chunk_at(c):
    return pl.ds(pl.multiple_of(c * CHUNK, CHUNK), CHUNK)


def alive_index(idx, c, first, lim):
    slots = first + c * CHUNK + lax.broadcasted_iota(jnp.int32, (1, CHUNK), 1)
    return jnp.where(slots < lim[0], idx[:, chunk_at(c)], -1)


def round_kernel(
    src, tgt, rel, sidx, tidx, kidx, lim, plan, inv,
    o_src, o_tgt, o_rel,
    raw, src_raw, low, table, heads, tails, kinds, query, head, tail, relrow, coef, gtail, ghead, grel, tg, sg,
    send1, recv1, send2, quarter, recv3, send4,
    t1, t2send, t2, half, halfin, halfx, rg, r1buf, r2buf, r2send, rax,
    sem_in, sem_loc, s1, r1, s2, r2, s3, r3, s4, r4, sag, rag, sbk, rbk, st, rt, srel, rrel,
):
    pc = Place()
    cin = pltpu.make_async_copy(tgt.at[:, lanes(pc.s)], raw, sem_in.at[0])
    cin.start()
    csrc = pltpu.make_async_copy(src, src_raw, sem_in.at[1])
    csrc.start()
    barrier = pc.greet()
    cin.wait()
    send1[...] = raw[...].astype(BF)
    pl.semaphore_wait(barrier, 66)
    leg_one(pc, send1, recv1, sem_loc.at[0], s1, r1)

    first = pc.s * EDGES
    r = rel[...]
    hi = r.astype(BF)
    mid = (r - hi.astype(F32)).astype(BF)
    lo = (r - hi.astype(F32) - mid.astype(F32)).astype(BF)
    rel3 = jnp.concatenate([hi, mid, lo], axis=0)
    csrc.wait()
    low[...] = src_raw[...].astype(BF)

    def gather_heads(c, carry):
        at = chunk_at(c)
        rows = lax.broadcasted_iota(jnp.int32, (ROWS, CHUNK), 0)
        hot = (rows == alive_index(sidx, c, first, lim)).astype(F32).astype(BF)
        heads[:, at] = hot
        h = dot(low[...], hot)
        head[:, at] = h.astype(BF)
        k16 = lax.broadcasted_iota(jnp.int32, (REL, CHUNK), 0)
        khot = (k16 == alive_index(kidx, c, first, lim)).astype(F32).astype(BF)
        kinds[:, at] = khot
        rr = dot(rel3, jnp.concatenate([khot, khot, khot], axis=0), 0, 0)
        relrow[:, at] = rr
        hr, hm, kr, km = h[:HALF], h[HALF:], rr[:HALF], rr[HALF:]
        query[:, at] = jnp.concatenate([hr * kr - hm * km, hr * km + hm * kr], axis=0).astype(BF)
        return carry

    lax.fori_loop(0, EDGES // CHUNK, gather_heads, 0)
    leg_one_wait(pc, send1, recv1, sem_loc.at[0], s1, r1)
    leg_two(pc, recv1, plan, send2, table, sem_loc.at[1], s2, r2)

    def mark_tails(c, carry):
        rows = lax.broadcasted_iota(jnp.int32, (ROWS, CHUNK), 0)
        tails[:, chunk_at(c)] = (rows == alive_index(tidx, c, first, lim)).astype(F32).astype(BF)
        return carry

    lax.fori_loop(0, EDGES // CHUNK, mark_tails, 0)
    leg_two_wait(pc, recv1, send2, table, sem_loc.at[1], s2, r2)

    def cp(out, q, c, o, i, ss, rs):
        ref = out.at[pl.ds(c * CHROWS, CHROWS), lanes(q)]
        return pltpu.make_async_remote_copy(
            src_ref=ref, dst_ref=ref, send_sem=ss.at[i, c], recv_sem=rs.at[i, c],
            device_id=(pc.me, o), device_id_type=MESH,
        )

    across = [cp(table, pc.s, c, pc.cross, 0, sag, rag) for c in range(CH)]
    beside = [cp(table, pc.s, c, pc.buddy, 1, sag, rag) for c in range(CH)]
    passed = [cp(table, pc.cross, c, pc.buddy, 2, sag, rag) for c in range(CH)]
    for c in range(CH):
        across[c].start()
        beside[c].start()
    for c in range(CH):
        beside[c].wait_recv()
    near = pl.ds(pl.multiple_of((pc.s // 2) * 512, 512), 512)
    far = pl.ds(pl.multiple_of((1 - pc.s // 2) * 512, 512), 512)

    def tails_near(c, carry):
        tail[:, chunk_at(c)] = dot(table[:, near], tails[near, chunk_at(c)]).astype(BF)
        return carry

    lax.fori_loop(0, EDGES // CHUNK, tails_near, 0)
    for c in range(CH):
        across[c].wait_recv()
        passed[c].start()
    for c in range(CH):
        passed[c].wait_recv()

    def tails_far(c, carry):
        at = chunk_at(c)
        tail[:, at] = (tail[:, at].astype(F32) + dot(table[:, far], tails[far, at])).astype(BF)
        return carry

    lax.fori_loop(0, EDGES // CHUNK, tails_far, 0)

    def score_span(k, carry):
        base = pl.multiple_of(k * E_CH, 128)
        at = pl.ds(base, E_CH)
        for b in range(E_CH // 128):
            qb = query[:, pl.ds(pl.multiple_of(base + 128 * b, 128), 128)]
            score = dot(qb, tail[:, at], 0, 0)
            for j in range(E_CH // 128):
                u = score[:, 128 * j:128 * j + 128]
                if j == b:
                    one = lax.broadcasted_iota(jnp.int32, (128, 128), 0) == lax.broadcasted_iota(jnp.int32, (128, 128), 1)
                    w = jax.nn.sigmoid(jnp.where(one, -u, u)) * jnp.where(one, -1.0, NEG_WEIGHT)
                else:
                    w = jax.nn.sigmoid(u) * NEG_WEIGHT
                coef[k, pl.ds(128 * b, 128), pl.ds(128 * j, 128)] = w.astype(BF)
        gtail[:, at] = dot(query[:, at], coef[k]).astype(BF)
        return carry

    lax.fori_loop(0, SPANS, score_span, 0)

    def rc(src_ref, dst_ref, i, o):
        return pltpu.make_async_remote_copy(
            src_ref=src_ref, dst_ref=dst_ref, send_sem=st.at[i], recv_sem=rt.at[i], device_id=(pc.me, o), device_id_type=MESH
        )

    def to_bucket(src_ref, dst_ref, i, p):
        return pltpu.make_async_remote_copy(
            src_ref=src_ref, dst_ref=dst_ref, send_sem=srel.at[i], recv_sem=rrel.at[i], device_id=(p, pc.s), device_id_type=MESH
        )

    def target_sum(q):
        tg[:, lanes(q)] = dot(gtail[...], tails[quarter_rows(q), :], 1, 1).astype(BF)

    ta = rc(tg.at[:, lanes(pc.diag)], t1.at[1], 0, pc.buddy)
    tb = rc(tg.at[:, lanes(pc.buddy)], t1.at[0], 1, pc.buddy)
    tc = rc(t2send, t2, 5, pc.cross)
    target_sum(pc.diag)
    ta.start()
    target_sum(pc.cross)
    ta.wait_recv()
    t2send[...] = (tg[:, lanes(pc.cross)].astype(F32) + t1[1].astype(F32)).astype(BF)
    tc.start()
    target_sum(pc.buddy)
    tb.start()
    target_sum(pc.s)

    def query_span(k, carry):
        at = pl.ds(pl.multiple_of(k * E_CH, 128), E_CH)
        gq = dot(tail[:, at], coef[k], 1, 1)
        gr, gm = gq[:HALF], gq[HALF:]
        rr = relrow[:, at]
        kr, km = rr[:HALF], rr[HALF:]
        h = head[:, at].astype(F32)
        hr, hm = h[:HALF], h[HALF:]
        ghead[:, at] = jnp.concatenate([gr * kr + gm * km, gm * kr - gr * km], axis=0).astype(BF)
        grel[:, at] = jnp.concatenate([gr * hr + gm * hm, gm * hr - gr * hm], axis=0).astype(BF)
        return carry

    lax.fori_loop(0, SPANS, query_span, 0)
    tb.wait_recv()
    tc.wait_recv()
    quarter[...] = (tg[:, lanes(pc.s)].astype(F32) + t1[0].astype(F32) + t2[...].astype(F32)).astype(BF)
    leg_one(pc, quarter, recv3, sem_loc.at[2], s3, r3)

    rg[:, 0:D] = dot(kinds[...], grel[...], 1, 1)
    rg[:, D:512] = jnp.zeros((REL, 512 - D), F32)
    ra = rc(rg, r1buf, 4, pc.buddy)
    ra.start()

    def source_sum(q):
        sg[:, lanes(q)] = dot(ghead[...], heads[quarter_rows(q), :], 1, 1).astype(BF)

    sa = rc(sg.at[:, lanes(pc.buddy)], halfin.at[0], 2, pc.buddy)
    sb = rc(sg.at[:, lanes(pc.diag)], halfin.at[1], 3, pc.buddy)
    source_sum(pc.buddy)
    sa.start()
    source_sum(pc.diag)
    sb.start()
    ra.wait_recv()
    r2send[...] = rg[...] + r1buf[...]
    rb = rc(r2send, r2buf, 6, pc.cross)
    rb.start()
    source_sum(pc.s)
    source_sum(pc.cross)

    leg_one_wait(pc, quarter, recv3, sem_loc.at[2], s3, r3)
    leg_two(pc, recv3, inv, send4, o_tgt, sem_loc.at[3], s4, r4)

    sc = rc(half.at[0], halfx.at[1], 7, pc.cross)
    sd = rc(half.at[1], halfx.at[0], 8, pc.cross)
    sa.wait_recv()
    half[0] = (sg[:, lanes(pc.s)].astype(F32) + halfin[0].astype(F32)).astype(BF)
    sc.start()
    sb.wait_recv()
    half[1] = (sg[:, lanes(pc.cross)].astype(F32) + halfin[1].astype(F32)).astype(BF)
    sd.start()
    rb.wait_recv()
    col = pl.ds(pl.multiple_of(pc.s * 128, 128), 128)
    px = [((pc.x + d) % 4) * 16 + pc.y * 4 + pc.z for d in (1, 2, 3)]
    py = [pc.x * 16 + ((pc.y + d) % 4) * 4 + pc.z for d in (1, 2, 3)]
    pz = [pc.x * 16 + pc.y * 4 + (pc.z + d) % 4 for d in (1, 2, 3)]

    def axis(i, coord, peers, total):
        rax[i, coord] = total
        for p in peers:
            to_bucket(rax.at[i, coord], rax.at[i, coord], i, p).start()

    def axis_wait(i, send=False):
        ref = rax.at[i, pl.ds(0, 3)]
        d = to_bucket(ref, ref, i, px[0])
        if send:
            d.wait_send()
            return None
        d.wait_recv()
        return (rax[i, 0] + rax[i, 1]) + (rax[i, 2] + rax[i, 3])

    axis(0, pc.x, px, r2send[:, col] + r2buf[:, col])
    axis(1, pc.y, py, axis_wait(0))
    axis(2, pc.z, pz, axis_wait(1))

    leg_two_wait(pc, recv3, send4, o_tgt, sem_loc.at[3], s4, r4)
    across2 = [cp(o_tgt, pc.s, c, pc.cross, 0, sbk, rbk) for c in range(CH)]
    beside2 = [cp(o_tgt, pc.s, c, pc.buddy, 1, sbk, rbk) for c in range(CH)]
    passed2 = [cp(o_tgt, pc.cross, c, pc.buddy, 2, sbk, rbk) for c in range(CH)]
    for c in range(CH):
        across2[c].start()
        beside2[c].start()

    o_rel[:, col] = axis_wait(2)
    rel_out = [rc(o_rel.at[:, col], o_rel.at[:, col], 11 + i, o) for i, o in enumerate((pc.buddy, pc.cross, pc.diag))]
    for c in rel_out:
        c.start()
    sc.wait_recv()
    sd.wait_recv()
    o_src[:, lanes(pc.s)] = (half[0].astype(F32) + halfx[0].astype(F32)).astype(BF)
    o_src[:, lanes(pc.cross)] = (half[1].astype(F32) + halfx[1].astype(F32)).astype(BF)
    se = rc(o_src.at[:, lanes(pc.s)], o_src.at[:, lanes(pc.s)], 9, pc.buddy)
    sf = rc(o_src.at[:, lanes(pc.cross)], o_src.at[:, lanes(pc.cross)], 10, pc.buddy)
    se.start()
    sf.start()
    for c in range(CH):
        across2[c].wait_recv()
        passed2[c].start()
    for c in range(CH):
        beside2[c].wait_recv()
        passed2[c].wait_recv()
    for c in (se, sf, *rel_out):
        c.wait_recv()

    for c in (ta, tb, tc, sa, sb, sc, sd, se, sf, ra, rb, *rel_out, *across, *beside, *passed, *across2, *beside2, *passed2):
        c.wait_send()
    for i in range(3):
        axis_wait(i, True)
    legs_sent(pc, recv1, s1, s2, r1)
    legs_sent(pc, recv3, s3, s4, r3)


def training_round(source_t, target_t, relation, sidx, tidx, kidx, counts, plan, inv):
    vm = pl.BlockSpec(memory_space=pltpu.VMEM)
    sm = pl.BlockSpec(memory_space=pltpu.SMEM)
    hb = pl.BlockSpec(memory_space=pl.ANY)
    dma = pltpu.SemaphoreType.DMA

    def bf(*shape):
        return pltpu.VMEM(shape, BF)

    def f(*shape):
        return pltpu.VMEM(shape, F32)

    tiles = bf(64, 16, 128)
    return pl.pallas_call(
        round_kernel,
        out_shape=(
            jax.ShapeDtypeStruct((D, ROWS), BF), jax.ShapeDtypeStruct((D, ROWS), BF), jax.ShapeDtypeStruct((REL, 512), F32),
        ),
        in_specs=[hb, hb, vm, vm, vm, vm, sm, sm, sm],
        out_specs=(vm, vm, vm),
        scratch_shapes=[
            f(D, Q), f(D, ROWS), bf(D, ROWS), bf(D, ROWS), bf(ROWS, EDGES), bf(ROWS, EDGES), bf(REL, EDGES),
            bf(D, EDGES), bf(D, EDGES), bf(D, EDGES), f(D, EDGES), bf(SPANS, E_CH, E_CH),
            bf(D, EDGES), bf(D, EDGES), bf(D, EDGES), bf(D, ROWS), bf(D, ROWS),
            bf(D, Q), tiles, tiles, bf(D, Q), tiles, tiles,
            bf(2, D, Q), bf(D, Q), bf(D, Q), bf(2, D, Q), bf(2, D, Q), bf(2, D, Q),
            f(REL, 512), f(REL, 512), f(REL, 512), f(REL, 512), f(3, 4, REL, 128),
            dma((2,)), dma((4,)), dma, dma, dma, dma, dma, dma, dma, dma,
            dma((3, CH)), dma((3, CH)), dma((3, CH)), dma((3, CH)), dma((14,)), dma((14,)), dma((3,)), dma((3,)),
        ],
        compiler_params=pltpu.CompilerParams(collective_id=0, has_side_effects=True, vmem_limit_bytes=56 << 20),
        name="training_round",
    )(source_t, target_t, relation, sidx, tidx, kidx, counts, plan, inv)


def adagrad_kernel(ws, ss, gs, wt, st, gt, wr, sr, gr, o_s, o_t, o_r):
    for w, s, g, o in ((ws, ss, gs, o_s), (wt, st, gt, o_t)):
        grad = g[...].astype(F32)
        total = s[...] + jnp.sum(grad * grad, axis=0, keepdims=True) * (1.0 / D)
        o[...] = w[...] - (LEARN_RATE * grad) / jnp.sqrt(total)

    @pl.when(pl.program_id(0) == 0)
    def _():
        grad = gr[:, 0:D]
        total = sr[...] + jnp.sum(grad * grad, axis=1, keepdims=True) * (1.0 / D)
        o_r[...] = wr[...] - (LEARN_RATE * grad) / jnp.sqrt(total)


def adagrad(ws, ss, gs, wt, st, gt, wr, sr, gr):
    n = 256
    tab = pl.BlockSpec((D, n), lambda i: (0, i))
    row = pl.BlockSpec((1, n), lambda i: (0, i))
    whole = lambda *s: pl.BlockSpec(s, lambda i: (0,) * len(s))
    return pl.pallas_call(
        adagrad_kernel,
        grid=(ROWS // n,),
        out_shape=(
            jax.ShapeDtypeStruct((D, ROWS), F32), jax.ShapeDtypeStruct((D, ROWS), F32), jax.ShapeDtypeStruct((REL, D), F32),
        ),
        in_specs=[tab, row, tab, tab, row, tab, whole(REL, D), whole(REL, 1), whole(REL, 512)],
        out_specs=(tab, tab, whole(REL, D)),
        compiler_params=pltpu.CompilerParams(vmem_limit_bytes=24 << 20),
        name="adagrad",
    )(ws, ss, gs, wt, st, gt, wr, sr, gr)


def per_device(source_table, target_table, source_state, target_state, relation, relation_state,
               plan, source_index, target_index, relation_index, edge_counts):
    source_t, target_t = source_table.T, target_table.T
    b = jnp.arange(64, dtype=jnp.int32)
    inv = jnp.sum(jnp.where(plan[None, :] == b[:, None], b[None, :], 0), axis=1)
    sg, tg, rg = training_round(
        source_t, target_t, relation, source_index, target_index, relation_index, edge_counts, plan, inv
    )
    ns, nt, nr = adagrad(
        source_t, source_state[None, :], sg, target_t, target_state[None, :], tg, relation, relation_state[:, None], rg
    )
    return ns.T, nt.T, nr


def solution(mesh):
    placed = (
        P("bucket", None), P("bucket", None), P("bucket"), P("bucket"), P(), P(), P(),
        P("bucket", "span"), P("bucket", "span"), P("bucket", "span"), P("bucket"),
    )
    return jax.shard_map(
        per_device,
        mesh=mesh,
        in_specs=placed,
        out_specs=(P("bucket", None), P("bucket", None), P()),
        check_vma=False,
    )
```

time: 117 us -> 99.4 us (0.85)
  Pallas kernels: 113 us -> 92.7 us
  other arithmetic: 0 us -> 1.28 us
    pallas_call x3 -> x1, Pallas kernels: 109 us -> 89.7 us  [training_round(): pl.pallas_call(round_kernel, out_shape=(jax.ShapeDtypeStruct((D, ROWS), B...]
    reduce_sum x0 -> x1, other arithmetic: none -> 1.28 us  [per_device(): inv = jnp.sum(jnp.where(plan[None, :] == b[:, None], b[None, :], 0), axis=1)]
    unnamed x20 -> x16, local copies, waits for them, and re-layouts: 2.13 us -> 3.06 us
where the time goes in v2:
time: 99.4 us; the launch traced here: 99.1 us
  Pallas kernels  92.7 us (93%)
  local copies, waits for them, and re-layouts  3.79 us (4%)
  between operations  1.35 us (1%)
  other arithmetic  1.28 us (1%)
    pallas_call x1, Pallas kernels, training_round(): pl.pallas_call(round_kernel, out_shape=(jax.ShapeDtypeStruct((D, ROWS), B...  89.7 us
    unnamed x16, local copies, waits for them, and re-layouts  3.06 us
    pallas_call x1, Pallas kernels, adagrad(): pl.pallas_call(adagrad_kernel, grid=(ROWS // n,), out_shape=(jax.ShapeDty...  3.01 us

profile of v2, /device:TPU:1, one launch (start us, length us, event | category | flops | bytes accessed | tf_op | source)
XLA Modules:
  0.0 99.1 jit_solution(17815876939978410202)
XLA Ops:
  1.3 1.3 %select_reduce_fusion.inv = s32[64]{0:T(128)} fusion(s32[64]{0:T(128)} %plan.1), kind=kLoop, calls=%fused_computation | loop fusion | flops 12224 | bytes 512 | tf_op jit(solution)/shard_map/reduce_sum | solution.py:495
  2.6 0.7 copy.15.sr
  3.3 0.0 copy-start
  3.3 0.0 copy-start.1
  3.3 0.0 copy-start.4
  3.3 0.0 copy-start.6
  3.3 0.0 copy-start.7
  3.3 89.7 %training_round.1 = (bf16[400,1024]{1,0:T(8,128)(2,1)}, bf16[400,1024]{1,0:T(8,128)(2,1)}, f32[16,512]{1,0:T(8,128)}) custom-call(f32[400,1024]{1,0:T(8,128)} %bitcast.7, f32[400,1024]{1,0:T(8,128)} %bitcast.9, f32[16,400]{1,0:T(8,128)} %wr.1, s32[1,2560]{1,0:T(1,128)} %sidx.1, s32[1,2560]{1,0:T(1,128)} %tidx.1, s32[1,2560]{1,0:T(1,128)} %kidx.1, ...), custom_call_target="tpu_custom_call" | custom-call | tf_op jit(solution)/shard_map/training_round/pallas_call | solution.py:438
  93.0 0.0 copy-done
  93.0 0.0 copy-done.1
  93.1 0.0 copy-done.4
  93.1 0.0 copy-done.6
  93.1 0.0 copy-done.7
  93.1 0.0 copy-start.2
  93.1 1.1 %copy-done.2 = bf16[400,1024]{1,0:T(8,128)(2,1)S(1)} copy-done((bf16[400,1024]{1,0:T(8,128)(2,1)S(1)}, bf16[400,1024]{1,0:T(8,128)(2,1)}, u32[]{:S(2)}) %copy-start.2) | copy-done | bytes 819224
  94.2 0.0 copy-start.3
  94.2 1.1 %copy-done.3 = bf16[400,1024]{1,0:T(8,128)(2,1)S(1)} copy-done((bf16[400,1024]{1,0:T(8,128)(2,1)S(1)}, bf16[400,1024]{1,0:T(8,128)(2,1)}, u32[]{:S(2)}) %copy-start.3) | copy-done | bytes 819224
  95.4 0.0 copy-start.5
  95.4 0.8 copy-done.5
  96.1 3.0 %adagrad.1 = (f32[400,1024]{1,0:T(8,128)}, f32[400,1024]{1,0:T(8,128)}, f32[16,400]{1,0:T(8,128)}) custom-call(f32[400,1024]{1,0:T(8,128)S(1)} %bitcast.8, f32[1,1024]{1,0:T(1,128)S(1)} %bitcast.11, bf16[400,1024]{1,0:T(8,128)(2,1)S(1)} %copy-done.2, f32[400,1024]{1,0:T(8,128)S(1)} %bitcast.10, f32[1,1024]{1,0:T(1,128)S(1)} %bitcast.12, ...), custom_call_target="tpu_custom_call" | custom-call | tf_op jit(solution)/shard_map/adagrad/pallas_call | solution.py:478
Async XLA Ops:
  3.3 89.7 %copy-start = (f32[1024,400]{0,1:T(8,128)S(1)}, f32[1024,400]{0,1:T(8,128)}, u32[]{:S(2)}) copy-start(f32[1024,400]{0,1:T(8,128)} %param.11) | copy-start | bytes 4915204
  3.3 89.8 %copy-start.1 = (f32[1024,400]{0,1:T(8,128)S(1)}, f32[1024,400]{0,1:T(8,128)}, u32[]{:S(2)}) copy-start(f32[1024,400]{0,1:T(8,128)} %param.12) | copy-start | bytes 4915204
  3.3 89.8 %copy-start.4 = (f32[16,400]{1,0:T(8,128)S(1)}, f32[16,400]{1,0:T(8,128)}, u32[]{:S(2)}) copy-start(f32[16,400]{1,0:T(8,128)} %wr.1) | copy-start | bytes 76804
  3.3 89.8 %copy-start.6 = (f32[1024]{0:T(1024)S(1)}, f32[1024]{0:T(1024)}, u32[]{:S(2)}) copy-start(f32[1024]{0:T(1024)} %param.13) | copy-start | bytes 12292
  3.3 89.8 %copy-start.7 = (f32[1024]{0:T(1024)S(1)}, f32[1024]{0:T(1024)}, u32[]{:S(2)}) copy-start(f32[1024]{0:T(1024)} %param.14) | copy-start | bytes 12292
  93.1 1.1 %copy-start.2 = (bf16[400,1024]{1,0:T(8,128)(2,1)S(1)}, bf16[400,1024]{1,0:T(8,128)(2,1)}, u32[]{:S(2)}) copy-start(bf16[400,1024]{1,0:T(8,128)(2,1)} %get-tuple-element.9.gs) | copy-start | bytes 2457604
  94.2 1.1 %copy-start.3 = (bf16[400,1024]{1,0:T(8,128)(2,1)S(1)}, bf16[400,1024]{1,0:T(8,128)(2,1)}, u32[]{:S(2)}) copy-start(bf16[400,1024]{1,0:T(8,128)(2,1)} %get-tuple-element.10.gt) | copy-start | bytes 2457604
  95.4 0.8 copy-start.5

commit v3 on v2

v3 whole, which is shorter than its diff:
```python
import functools

import jax
import jax.numpy as jnp
from jax import lax
from jax.experimental import pallas as pl
from jax.experimental.pallas import tpu as pltpu
from jax.sharding import PartitionSpec as P

MESH = pl.DeviceIdType.MESH
BF = jnp.bfloat16
F32 = jnp.float32
E_CH = 640
LEARN_RATE = 0.25
NEG_WEIGHT = 0.03125
D = 400
HALF = 200
ROWS = 1024
Q = 256
EDGES = 2560
SPANS = 4
REL = 16
TILES = 50
CH = 5
CHROWS = D // CH
CHUNK = 512


class Place:
    def __init__(self):
        rem, div = lax.rem, lax.div
        self.me = lax.axis_index("bucket")
        self.s = lax.axis_index("span")
        self.x = div(self.me, 16)
        self.y = rem(div(self.me, 4), 4)
        self.z = rem(self.me, 4)
        self.zl = div(self.s, 2)
        self.core = rem(self.s, 2)
        self.buddy = self.s + 1 - 2 * self.core
        self.cross = rem(self.s + 2, 4)
        self.diag = rem(self.buddy + 2, 4)
        self.X = [rem(self.x + d, 4) for d in range(4)]
        self.Y = [rem(self.y + d, 4) for d in range(4)]
        self.Z = [rem(self.z + d, 4) for d in range(4)]
        way = 2 * self.zl - 1
        height = 2 * self.z + self.zl
        self.H = [rem(height + way * d + 8, 8) for d in range(4)]
        self.hz = [div(h, 2) for h in self.H]
        self.hs = [2 * rem(h, 2) + self.core for h in self.H]
        self.odd = [rem(d + 1 + self.zl, 2) for d in range(4)]
        self.U = [[rem(x + 2 * self.core + h, 4) for x in self.X] for h in self.H]
        self.row = 128 * self.U[0][0] + 32 * self.y + 16 * self.odd[0]
        self.relay = jnp.logical_or(self.U[0][0] < 3, jnp.logical_and(self.y == 0, self.odd[0] == 0))
        self.ds = [self.s, self.core, 2 - 2 * self.zl + self.core, 2 + self.core]
        self.dk = [0, 1 - self.zl, 1, self.zl]

    def greet(self):
        barrier = pltpu.get_barrier_semaphore()

        def hello(bucket, span):
            pl.semaphore_signal(barrier, inc=1, device_id=(bucket, span), device_id_type=MESH)

        beyond = rem8_pair(self)
        for dx in range(4):
            for dy in range(4):
                part = 16 * self.X[dx] + 4 * self.Y[dy]
                for d in range(4):
                    if dx or dy or d:
                        hello(part + self.hz[d], self.hs[d])
                hello(part + beyond, self.s)
        for o in (self.buddy, self.cross, self.diag):
            hello(self.me, o)
        hello(16 * self.x + 4 * self.y + self.Z[2], self.s)
        return barrier


GREETED = 63 + 16 + 3 + 1


def rem8_pair(pc):
    return lax.rem(pc.z + 1 + 2 * pc.zl, 4)


STEPS = (0, 1, 2, 1)
FAR_FIRST = sorted(
    ((dx, dy, d) for dx in range(4) for dy in range(4) for d in range(4)),
    key=lambda o: -(STEPS[o[0]] + STEPS[o[1]] + o[2]),
)


def tile_at(ref, row, lane):
    return ref.at[pl.ds(pl.multiple_of(row, 16), 16), pl.ds(pl.multiple_of(lane, 128), 128)]


def wait_tiles(buf, n, ssem, rsem, pc, send):
    ref = buf.at[pl.ds(0, n)]
    d = pltpu.make_async_remote_copy(
        src_ref=ref, dst_ref=ref, send_sem=ssem, recv_sem=rsem, device_id=(pc.me, pc.buddy), device_id_type=MESH
    )
    if send:
        d.wait_send()
    else:
        d.wait_recv()


def leg_one(pc, src, recv, sem_loc, ssem, rsem):
    for dx, dy, d in FAR_FIRST:
        if not (dx or dy or d):
            continue
        u = pc.U[d][dx]

        @pl.when(jnp.logical_or(u < 3, jnp.logical_and(pc.Y[dy] == 0, pc.odd[d] == 0)))
        def _():
            pltpu.make_async_remote_copy(
                src_ref=tile_at(src, 128 * u + 32 * pc.Y[dy] + 16 * pc.odd[d], 128 * (d // 2)),
                dst_ref=recv.at[pc.me], send_sem=ssem, recv_sem=rsem,
                device_id=(16 * pc.X[dx] + 4 * pc.Y[dy] + pc.hz[d], pc.hs[d]), device_id_type=MESH,
            ).start()

    @pl.when(pc.relay)
    def _():
        pltpu.make_async_copy(tile_at(src, pc.row, 0), recv.at[pc.me], sem_loc).start()


def leg_one_wait(pc, src, recv, sem_loc, ssem, rsem):
    @pl.when(pc.relay)
    def _():
        pltpu.make_async_copy(tile_at(src, pc.row, 0), recv.at[pc.me], sem_loc).wait()
        wait_tiles(recv, 63, ssem, rsem, pc, False)


def leg_two(pc, recv, pick, send, dst, sem_loc, ssem, rsem):
    @pl.when(pc.relay)
    def _():
        for i in range(64):
            send[i] = recv[pick(i)]
        for dx, dy, e in FAR_FIRST:
            if dx or dy or e:
                p = 16 * pc.X[dx] + 4 * pc.Y[dy] + pc.Z[e]
                pltpu.make_async_remote_copy(
                    src_ref=send.at[p], dst_ref=tile_at(dst, pc.row, Q * pc.ds[e] + 128 * pc.dk[e]),
                    send_sem=ssem, recv_sem=rsem, device_id=(p, pc.ds[e]), device_id_type=MESH,
                ).start()
        pltpu.make_async_copy(send.at[pc.me], tile_at(dst, pc.row, Q * pc.s), sem_loc).start()


def leg_two_wait(pc, recv, send, dst, sem_loc, ssem, rsem):
    @pl.when(pc.relay)
    def _():
        pltpu.make_async_copy(send.at[pc.me], tile_at(dst, pc.row, Q * pc.s), sem_loc).wait()
        wait_tiles(recv, TILES - 1, ssem, rsem, pc, False)

    @pl.when(jnp.logical_not(pc.relay))
    def _():
        wait_tiles(recv, TILES, ssem, rsem, pc, False)


def legs_sent(pc, recv, s1, s2, r1):
    @pl.when(pc.relay)
    def _():
        wait_tiles(recv, TILES - 1, s1, r1, pc, True)
        wait_tiles(recv, 63, s2, r1, pc, True)

    @pl.when(jnp.logical_not(pc.relay))
    def _():
        wait_tiles(recv, TILES, s1, r1, pc, True)


def lanes(q, n=Q):
    return pl.ds(pl.multiple_of(q * Q, Q), n)


def dot(a, b, ca=1, cb=0):
    return lax.dot_general(a, b, (((ca,), (cb,)), ((), ())), preferred_element_type=F32)


def quarter_rows(q):
    return pl.ds(pl.multiple_of(q * Q, Q), Q)


def chunk_at(c):
    return pl.ds(c * CHUNK if isinstance(c, int) else pl.multiple_of(c * CHUNK, CHUNK), CHUNK)


def alive_index(index, c, first, lim):
    slots = first + c * CHUNK + lax.broadcasted_iota(jnp.int32, (1, CHUNK), 1)
    return jnp.where(slots < lim[0], index, -1)


def group_column(core, g, z):
    t = lax.rem(g - z + 4, 4)
    upper = jnp.logical_and(t > 0, t < 3).astype(jnp.int32)
    second = (t > 1).astype(jnp.int32)
    return 4 * upper + 2 * core + second


def place_of_row(row, z):
    return 128 * group_column(row // 512, (row // 128) % 4, z) + row % 128


def round_kernel(
    src, tgt, rel_in, sidx_in, tidx_in, kidx_in, planrow_in, lim_in, plan_in,
    o_src, o_tgt, o_rel,
    rel, sidx, tidx, kidx, planrow, lim, plan,
    raw, src_raw, low, table, heads, tails, kinds, query, head, tail, relrow, coef, gtail, ghead, grel, tg, sg,
    send1, recv1, send2, quarter, recv3, send4,
    t1, t2send, t2, half, halfin, halfx, rg, r1buf, r2buf, r2send, rax, invcol, inv,
    sem_in, sem_loc, s1, r1, s2, r2, s3, r3, s4, r4, sag, rag, sbk, rbk, st, rt, srel, rrel,
):
    pc = Place()
    cin = []
    for k in range(2):
        g = lax.rem(pc.z + pc.zl + 3 * k - 2 * k * pc.zl, 4)
        at = pl.ds(pl.multiple_of(512 * pc.core + 128 * g, 128), 128)
        cin.append(pltpu.make_async_copy(tgt.at[:, at], raw.at[:, pl.ds(128 * k, 128)], sem_in.at[3 + k]))
    small = [
        pltpu.make_async_copy(a, b, sem_in.at[5 + i]) for i, (a, b) in enumerate((
            (rel_in, rel), (sidx_in, sidx), (tidx_in, tidx), (kidx_in, kidx), (planrow_in, planrow), (lim_in, lim), (plan_in, plan),
        ))
    ]
    csrc = pltpu.make_async_copy(src, src_raw, sem_in.at[1])
    for c in (*cin, *small, csrc):
        c.start()
    barrier = pc.greet()
    for c in cin:
        c.wait()
    send1[...] = raw[...].astype(BF)
    pl.semaphore_wait(barrier, GREETED)
    leg_one(pc, send1, recv1, sem_loc.at[0], s1, r1)

    first = pc.s * EDGES
    for c in small:
        c.wait()
    r = rel[...]
    hi = r.astype(BF)
    mid = (r - hi.astype(F32)).astype(BF)
    lo = (r - hi.astype(F32) - mid.astype(F32)).astype(BF)
    rel3 = jnp.concatenate([hi, mid, lo], axis=0)
    here = lax.broadcasted_iota(jnp.int32, (64, 64), 0) == planrow[...]
    found = jnp.sum(jnp.where(here, lax.broadcasted_iota(jnp.int32, (64, 64), 1), 0), axis=1, keepdims=True)
    invcol[...] = jnp.broadcast_to(jnp.minimum(found, 63), (64, 128))
    cinv = pltpu.make_async_copy(invcol, inv, sem_in.at[2])
    cinv.start()
    csrc.wait()
    low[...] = src_raw[...].astype(BF)

    def gather_heads(c, carry):
        at = chunk_at(c)
        rows = lax.broadcasted_iota(jnp.int32, (ROWS, CHUNK), 0)
        hot = (rows == alive_index(sidx[:, at], c, first, lim)).astype(F32).astype(BF)
        heads[:, at] = hot
        h = dot(low[...], hot)
        head[:, at] = h.astype(BF)
        k16 = lax.broadcasted_iota(jnp.int32, (REL, CHUNK), 0)
        khot = (k16 == alive_index(kidx[:, at], c, first, lim)).astype(F32).astype(BF)
        kinds[:, at] = khot
        rr = dot(rel3, jnp.concatenate([khot, khot, khot], axis=0), 0, 0)
        relrow[:, at] = rr
        hr, hm, kr, km = h[:HALF], h[HALF:], rr[:HALF], rr[HALF:]
        query[:, at] = jnp.concatenate([hr * kr - hm * km, hr * km + hm * kr], axis=0).astype(BF)
        return carry

    lax.fori_loop(0, EDGES // CHUNK, gather_heads, 0)
    cinv.wait()
    leg_one_wait(pc, send1, recv1, sem_loc.at[0], s1, r1)
    leg_two(pc, recv1, lambda i: plan[i], send2, table, sem_loc.at[1], s2, r2)

    def mark_tails(c, carry):
        rows = lax.broadcasted_iota(jnp.int32, (ROWS, CHUNK), 0)
        tails[:, chunk_at(c)] = (rows == alive_index(place_of_row(tidx[:, chunk_at(c)], pc.z), c, first, lim)).astype(F32).astype(BF)
        return carry

    lax.fori_loop(0, EDGES // CHUNK, mark_tails, 0)
    leg_two_wait(pc, recv1, send2, table, sem_loc.at[1], s2, r2)

    def cp(out, q, c, o, i, ss, rs):
        ref = out.at[pl.ds(c * CHROWS, CHROWS), lanes(q)]
        return pltpu.make_async_remote_copy(
            src_ref=ref, dst_ref=ref, send_sem=ss.at[i, c], recv_sem=rs.at[i, c],
            device_id=(pc.me, o), device_id_type=MESH,
        )

    across = [cp(table, pc.s, c, pc.cross, 0, sag, rag) for c in range(CH)]
    beside = [cp(table, pc.s, c, pc.buddy, 1, sag, rag) for c in range(CH)]
    passed = [cp(table, pc.cross, c, pc.buddy, 2, sag, rag) for c in range(CH)]
    for c in range(CH):
        across[c].start()
        beside[c].start()
    for c in range(CH):
        beside[c].wait_recv()
    near = pl.ds(pl.multiple_of(pc.zl * 512, 512), 512)
    far = pl.ds(pl.multiple_of(512 - pc.zl * 512, 512), 512)

    def tails_near(c, carry):
        tail[:, chunk_at(c)] = dot(table[:, near], tails[near, chunk_at(c)]).astype(BF)
        return carry

    for c in range(EDGES // CHUNK):
        tails_near(c, 0)
    for c in range(CH):
        across[c].wait_recv()
        passed[c].start()
    for c in range(CH):
        passed[c].wait_recv()

    def tails_far(c, carry):
        at = chunk_at(c)
        tail[:, at] = (tail[:, at].astype(F32) + dot(table[:, far], tails[far, at])).astype(BF)
        return carry

    for c in range(EDGES // CHUNK):
        tails_far(c, 0)

    def score_span(k, carry):
        base = pl.multiple_of(k * E_CH, 128)
        at = pl.ds(base, E_CH)
        for b in range(E_CH // 128):
            qb = query[:, pl.ds(pl.multiple_of(base + 128 * b, 128), 128)]
            score = dot(qb, tail[:, at], 0, 0)
            for j in range(E_CH // 128):
                u = score[:, 128 * j:128 * j + 128]
                if j == b:
                    one = lax.broadcasted_iota(jnp.int32, (128, 128), 0) == lax.broadcasted_iota(jnp.int32, (128, 128), 1)
                    w = jax.nn.sigmoid(jnp.where(one, -u, u)) * jnp.where(one, -1.0, NEG_WEIGHT)
                else:
                    w = jax.nn.sigmoid(u) * NEG_WEIGHT
                coef[k, pl.ds(128 * b, 128), pl.ds(128 * j, 128)] = w.astype(BF)
        gtail[:, at] = dot(query[:, at], coef[k]).astype(BF)
        return carry

    lax.fori_loop(0, SPANS, score_span, 0)

    def rc(src_ref, dst_ref, i, o):
        return pltpu.make_async_remote_copy(
            src_ref=src_ref, dst_ref=dst_ref, send_sem=st.at[i], recv_sem=rt.at[i], device_id=(pc.me, o), device_id_type=MESH
        )

    def to_bucket(src_ref, dst_ref, i, p):
        return pltpu.make_async_remote_copy(
            src_ref=src_ref, dst_ref=dst_ref, send_sem=srel.at[i], recv_sem=rrel.at[i], device_id=(p, pc.s), device_id_type=MESH
        )

    def target_sum(part):
        tg[:, part] = dot(gtail[...], tails[part, :], 1, 1).astype(BF)

    ta = rc(tg.at[:, lanes(pc.diag)], t1.at[1], 0, pc.buddy)
    tb = rc(tg.at[:, lanes(pc.buddy)], t1.at[0], 1, pc.buddy)
    tc = rc(t2send, t2, 5, pc.cross)
    target_sum(far)
    ta.start()
    target_sum(near)
    tb.start()
    ta.wait_recv()
    t2send[...] = (tg[:, lanes(pc.cross)].astype(F32) + t1[1].astype(F32)).astype(BF)
    tc.start()
    def query_span(k, carry):
        at = pl.ds(pl.multiple_of(k * E_CH, 128), E_CH)
        gq = dot(tail[:, at], coef[k], 1, 1)
        gr, gm = gq[:HALF], gq[HALF:]
        rr = relrow[:, at]
        kr, km = rr[:HALF], rr[HALF:]
        h = head[:, at].astype(F32)
        hr, hm = h[:HALF], h[HALF:]
        ghead[:, at] = jnp.concatenate([gr * kr + gm * km, gm * kr - gr * km], axis=0).astype(BF)
        grel[:, at] = jnp.concatenate([gr * hr + gm * hm, gm * hr - gr * hm], axis=0).astype(BF)
        return carry

    lax.fori_loop(0, SPANS, query_span, 0)

    def source_sum(part):
        sg[:, part] = dot(ghead[...], heads[part, :], 1, 1).astype(BF)

    sa = rc(sg.at[:, lanes(pc.buddy)], halfin.at[0], 2, pc.buddy)
    sb = rc(sg.at[:, lanes(pc.diag)], halfin.at[1], 3, pc.buddy)
    ra = rc(rg, r1buf, 4, pc.buddy)
    rg[:, 0:D] = dot(kinds[...], grel[...], 1, 1)
    rg[:, D:512] = jnp.zeros((REL, 512 - D), F32)
    ra.start()
    source_sum(near)
    sa.start()
    tb.wait_recv()
    tc.wait_recv()
    quarter[...] = (tg[:, lanes(pc.s)].astype(F32) + t1[0].astype(F32) + t2[...].astype(F32)).astype(BF)
    leg_one(pc, quarter, recv3, sem_loc.at[2], s3, r3)

    ra.wait_recv()
    r2send[...] = rg[...] + r1buf[...]
    rb = rc(r2send, r2buf, 6, pc.cross)
    rb.start()
    sc = rc(half.at[0], halfx.at[1], 7, pc.cross)
    sd = rc(half.at[1], halfx.at[0], 8, pc.cross)
    sa.wait_recv()
    half[0] = (sg[:, lanes(pc.s)].astype(F32) + halfin[0].astype(F32)).astype(BF)
    sc.start()
    source_sum(far)
    sb.start()
    sb.wait_recv()
    half[1] = (sg[:, lanes(pc.cross)].astype(F32) + halfin[1].astype(F32)).astype(BF)

    col = pl.ds(pl.multiple_of(pc.s * 128, 128), 128)
    px = [16 * x + 4 * pc.y + pc.z for x in pc.X[1:]]
    py = [16 * pc.x + 4 * y + pc.z for y in pc.Y[1:]]
    pz = [16 * pc.x + 4 * pc.y + z for z in pc.Z[1:]]

    def axis(i, coord, peers, total):
        rax[i, coord] = total
        for p in peers:
            to_bucket(rax.at[i, coord], rax.at[i, coord], i, p).start()

    def axis_wait(i, send=False):
        ref = rax.at[i, pl.ds(0, 3)]
        d = to_bucket(ref, ref, i, px[0])
        if send:
            d.wait_send()
            return None
        d.wait_recv()
        return (rax[i, 0] + rax[i, 1]) + (rax[i, 2] + rax[i, 3])

    rb.wait_recv()
    axis(0, pc.x, px, r2send[:, col] + r2buf[:, col])
    leg_one_wait(pc, quarter, recv3, sem_loc.at[2], s3, r3)
    leg_two(pc, recv3, lambda i: inv[i, 0], send4, o_tgt, sem_loc.at[3], s4, r4)
    sd.start()
    axis(1, pc.y, py, axis_wait(0))
    axis(2, pc.z, pz, axis_wait(1))

    leg_two_wait(pc, recv3, send4, o_tgt, sem_loc.at[3], s4, r4)
    across2 = [cp(o_tgt, pc.s, c, pc.cross, 0, sbk, rbk) for c in range(CH)]
    beside2 = [cp(o_tgt, pc.s, c, pc.buddy, 1, sbk, rbk) for c in range(CH)]
    passed2 = [cp(o_tgt, pc.cross, c, pc.buddy, 2, sbk, rbk) for c in range(CH)]
    for c in range(CH):
        across2[c].start()
        beside2[c].start()

    sc.wait_recv()
    sd.wait_recv()
    o_src[:, lanes(pc.s)] = (half[0].astype(F32) + halfx[0].astype(F32)).astype(BF)
    o_src[:, lanes(pc.cross)] = (half[1].astype(F32) + halfx[1].astype(F32)).astype(BF)
    se = rc(o_src.at[:, lanes(pc.s)], o_src.at[:, lanes(pc.s)], 9, pc.buddy)
    sf = rc(o_src.at[:, lanes(pc.cross)], o_src.at[:, lanes(pc.cross)], 10, pc.buddy)
    se.start()
    sf.start()
    for c in range(CH):
        across2[c].wait_recv()
        passed2[c].start()
    o_rel[:, col] = axis_wait(2)
    rel_out = [rc(o_rel.at[:, col], o_rel.at[:, col], 11 + i, o) for i, o in enumerate((pc.buddy, pc.cross, pc.diag))]
    for c in rel_out:
        c.start()
    for c in range(CH):
        beside2[c].wait_recv()
        passed2[c].wait_recv()
    for c in (se, sf, *rel_out):
        c.wait_recv()

    for c in (ta, tb, tc, sa, sb, sc, sd, se, sf, ra, rb, *rel_out, *across, *beside, *passed, *across2, *beside2, *passed2):
        c.wait_send()
    for i in range(3):
        axis_wait(i, True)
    legs_sent(pc, recv1, s1, s2, r1)
    legs_sent(pc, recv3, s3, s4, r3)


def training_round(source_t, target_t, relation, sidx, tidx, kidx, counts, plan):
    vm = pl.BlockSpec(memory_space=pltpu.VMEM)
    hb = pl.BlockSpec(memory_space=pltpu.HBM)
    dma = pltpu.SemaphoreType.DMA

    def i32(*shape):
        return pltpu.VMEM(shape, jnp.int32)

    def bf(*shape):
        return pltpu.VMEM(shape, BF)

    def f(*shape):
        return pltpu.VMEM(shape, F32)

    tiles = bf(64, 16, 128)
    kept = [
        pltpu.with_memory_space_constraint(a, pltpu.HBM) for a in (source_t, target_t, relation, sidx, tidx, kidx, plan[None, :])
    ]
    return pl.pallas_call(
        round_kernel,
        out_shape=(
            jax.ShapeDtypeStruct((D, ROWS), BF), jax.ShapeDtypeStruct((D, ROWS), BF), jax.ShapeDtypeStruct((REL, 512), F32),
        ),
        in_specs=[hb] * 9,
        out_specs=(vm, vm, vm),
        scratch_shapes=[
            f(REL, D), i32(1, EDGES), i32(1, EDGES), i32(1, EDGES), i32(1, 64), pltpu.SMEM((1,), jnp.int32), pltpu.SMEM((64,), jnp.int32),
            f(D, Q), f(D, ROWS), bf(D, ROWS), bf(D, ROWS), bf(ROWS, EDGES), bf(ROWS, EDGES), bf(REL, EDGES),
            bf(D, EDGES), bf(D, EDGES), bf(D, EDGES), f(D, EDGES), bf(SPANS, E_CH, E_CH),
            bf(D, EDGES), bf(D, EDGES), bf(D, EDGES), bf(D, ROWS), bf(D, ROWS),
            bf(D, Q), tiles, tiles, bf(D, Q), tiles, tiles,
            bf(2, D, Q), bf(D, Q), bf(D, Q), bf(2, D, Q), bf(2, D, Q), bf(2, D, Q),
            f(REL, 512), f(REL, 512), f(REL, 512), f(REL, 512), f(3, 4, REL, 128),
            pltpu.VMEM((64, 128), jnp.int32), pltpu.SMEM((64, 128), jnp.int32),
            dma((12,)), dma((4,)), dma, dma, dma, dma, dma, dma, dma, dma,
            dma((3, CH)), dma((3, CH)), dma((3, CH)), dma((3, CH)), dma((14,)), dma((14,)), dma((3,)), dma((3,)),
        ],
        compiler_params=pltpu.CompilerParams(collective_id=0, has_side_effects=True, vmem_limit_bytes=46 << 20),
        name="training_round",
    )(*kept, counts, pltpu.with_memory_space_constraint(plan, pltpu.HBM))


def adagrad_kernel(ws, ss, gs, wt, st, gt, wr, sr, gr, o_s, o_t, o_r, buf, sem):
    copies = []
    z = lax.rem(lax.axis_index("bucket"), 4)
    for i, (w, s, g, o) in enumerate(((ws, ss, gs, o_s), (wt, st, gt, o_t))):
        for q in range(ROWS // Q):
            at = pl.ds(q * Q, Q)
            if i == 0:
                grad = g[:, at].astype(F32)
            else:
                cols = [pl.multiple_of(128 * group_column(q // 2, 2 * (q % 2) + h, z), 128) for h in range(2)]
                grad = jnp.concatenate([g[:, pl.ds(c, 128)] for c in cols], axis=1).astype(F32)
            total = s[:, at] + jnp.sum(grad * grad, axis=0, keepdims=True) * (1.0 / D)
            buf[i, q] = w[:, at] - (LEARN_RATE * grad) / jnp.sqrt(total)
            copies.append(pltpu.make_async_copy(buf.at[i, q], o.at[:, at], sem.at[i, q]))
            copies[-1].start()
    grad = gr[:, 0:D]
    same = lax.broadcasted_iota(jnp.int32, (REL, REL), 0) == lax.broadcasted_iota(jnp.int32, (REL, REL), 1)
    state = jnp.sum(jnp.where(same, sr[...], 0.0), axis=1, keepdims=True)
    total = state + jnp.sum(grad * grad, axis=1, keepdims=True) * (1.0 / D)
    o_r[...] = wr[...] - (LEARN_RATE * grad) / jnp.sqrt(total)
    for c in copies:
        c.wait()


def adagrad(*args):
    vm = pl.BlockSpec(memory_space=pltpu.VMEM)
    hb = pl.BlockSpec(memory_space=pl.ANY)
    return pl.pallas_call(
        adagrad_kernel,
        out_shape=(
            jax.ShapeDtypeStruct((D, ROWS), F32), jax.ShapeDtypeStruct((D, ROWS), F32), jax.ShapeDtypeStruct((REL, D), F32),
        ),
        in_specs=[vm] * 9,
        out_specs=(hb, hb, vm),
        scratch_shapes=[pltpu.VMEM((2, ROWS // Q, D, Q), F32), pltpu.SemaphoreType.DMA((2, ROWS // Q))],
        compiler_params=pltpu.CompilerParams(vmem_limit_bytes=24 << 20),
        name="adagrad",
    )(*args)


def per_device(source_table, target_table, source_state, target_state, relation, relation_state,
               plan, source_index, target_index, relation_index, edge_counts):
    source_t, target_t = source_table.T, target_table.T
    sg, tg, rg = training_round(
        source_t, target_t, relation, source_index, target_index, relation_index, edge_counts, plan
    )
    ns, nt, nr = adagrad(
        source_t, source_state[None, :], sg, target_t, target_state[None, :], tg, relation, relation_state[None, :], rg
    )
    return ns.T, nt.T, nr


def solution(mesh):
    placed = (
        P("bucket", None), P("bucket", None), P("bucket"), P("bucket"), P(), P(), P(),
        P("bucket", "span"), P("bucket", "span"), P("bucket", "span"), P("bucket"),
    )
    return jax.shard_map(
        per_device,
        mesh=mesh,
        in_specs=placed,
        out_specs=(P("bucket", None), P("bucket", None), P()),
        check_vma=False,
    )
```

time: 99.4 us -> 82 us (0.82)
  Pallas kernels: 92.7 us -> 80.5 us
  local copies, waits for them, and re-layouts: 3.79 us -> 0.03 us
  other arithmetic: 1.28 us -> 0 us
    pallas_call x1, Pallas kernels: 89.7 us -> 77.3 us  [training_round(): pl.pallas_call(round_kernel, out_shape=(jax.ShapeDtypeStruct((D, ROWS), B...]
    unnamed x16 -> x12, local copies, waits for them, and re-layouts: 3.06 us -> 0.03 us
    reduce_sum x1 -> x0, other arithmetic: 1.28 us -> none  [per_device(): inv = jnp.sum(jnp.where(plan[None, :] == b[:, None], b[None, :], 0), axis=1)]
where the time goes in v3:
time: 82 us; the launch traced here: 81.9 us
  Pallas kernels  80.5 us (98%)
  between operations  1.38 us (2%)
    pallas_call x1, Pallas kernels, training_round(): pl.pallas_call(round_kernel, out_shape=(jax.ShapeDtypeStruct((D, ROWS), B...  77.3 us
    pallas_call x1, Pallas kernels, adagrad(): pl.pallas_call(adagrad_kernel, out_shape=(jax.ShapeDtypeStruct((D, ROWS),...  3.18 us

profile of v3, /device:TPU:1, one launch (start us, length us, event | category | flops | bytes accessed | tf_op | source)
XLA Modules:
  0.0 81.9 jit_solution(6542027499075184860)
XLA Ops:
  1.3 0.0 copy-start
  1.3 0.0 copy-start.1
  1.3 0.0 copy-start.2
  1.3 0.0 copy-start.3
  1.3 0.0 copy-start.4
  1.3 0.0 copy-start.5
  1.3 77.3 %training_round.1 = (bf16[400,1024]{1,0:T(8,128)(2,1)S(1)}, bf16[400,1024]{1,0:T(8,128)(2,1)S(1)}, f32[16,512]{1,0:T(8,128)S(1)}) custom-call(f32[400,1024]{1,0:T(8,128)} %bitcast.8, f32[400,1024]{1,0:T(8,128)} %bitcast.10, f32[16,400]{1,0:T(8,128)} %wr.1, s32[1,2560]{1,0:T(1,128)} %sidx_in.1, s32[1,2560]{1,0:T(1,128)} %tidx_in.1, s32[1,2560]{1,0:T(1,128)} %kidx_in.1, ...), custom_call_target="tpu_custom_call" | custom-call | tf_op jit(solution)/shard_map/training_round/pallas_call | solution.py:482
  78.6 0.0 copy-done
  78.7 0.0 copy-done.1
  78.7 0.0 copy-done.2
  78.7 0.0 copy-done.3
  78.7 0.0 copy-done.4
  78.7 0.0 copy-done.5
  78.7 3.2 %adagrad.1 = (f32[400,1024]{1,0:T(8,128)}, f32[400,1024]{1,0:T(8,128)}, f32[16,400]{1,0:T(8,128)}) custom-call(f32[400,1024]{1,0:T(8,128)S(1)} %bitcast.9, f32[1,1024]{1,0:T(1,128)S(1)} %bitcast.12, bf16[400,1024]{1,0:T(8,128)(2,1)S(1)} %get-tuple-element.9.gs, f32[400,1024]{1,0:T(8,128)S(1)} %bitcast.11, f32[1,1024]{1,0:T(1,128)S(1)} %bitcast.13, ...), custom_call_target="tpu_custom_call" | custom-call | tf_op jit(solution)/shard_map/adagrad/pallas_call | solution.py:533
Async XLA Ops:
  1.3 77.4 %copy-start = (f32[1024,400]{0,1:T(8,128)S(1)}, f32[1024,400]{0,1:T(8,128)}, u32[]{:S(2)}) copy-start(f32[1024,400]{0,1:T(8,128)} %param.11) | copy-start | bytes 4915204
  1.3 77.4 %copy-start.1 = (f32[1024,400]{0,1:T(8,128)S(1)}, f32[1024,400]{0,1:T(8,128)}, u32[]{:S(2)}) copy-start(f32[1024,400]{0,1:T(8,128)} %param.12) | copy-start | bytes 4915204
  1.3 77.4 %copy-start.2 = (f32[16,400]{1,0:T(8,128)S(1)}, f32[16,400]{1,0:T(8,128)}, u32[]{:S(2)}) copy-start(f32[16,400]{1,0:T(8,128)} %wr.1) | copy-start | bytes 76804
  1.3 77.4 %copy-start.3 = (f32[1024]{0:T(1024)S(1)}, f32[1024]{0:T(1024)}, u32[]{:S(2)}) copy-start(f32[1024]{0:T(1024)} %param.13) | copy-start | bytes 12292
  1.3 77.4 %copy-start.4 = (f32[1024]{0:T(1024)S(1)}, f32[1024]{0:T(1024)}, u32[]{:S(2)}) copy-start(f32[1024]{0:T(1024)} %param.14) | copy-start | bytes 12292
  1.3 77.4 %copy-start.5 = (f32[16]{0:T(128)S(1)}, f32[16]{0:T(128)}, u32[]{:S(2)}) copy-start(f32[16]{0:T(128)} %param.16) | copy-start | bytes 196

commit v4 on v3

--- a/solution.py
+++ b/solution.py
@@ -21,8 +21,8 @@
 SPANS = 4
 REL = 16
 TILES = 50
-CH = 5
-CHROWS = D // CH
+PIECES = ((0, 0, 208), (0, 208, 192), (1, 0, 208), (1, 208, 192))
+CH = len(PIECES)
 CHUNK = 512
 
 
@@ -61,12 +61,11 @@
             pl.semaphore_signal(barrier, inc=1, device_id=(bucket, span), device_id_type=MESH)
 
         beyond = rem8_pair(self)
-        for dx in range(4):
-            for dy in range(4):
-                part = 16 * self.X[dx] + 4 * self.Y[dy]
-                for d in range(4):
-                    if dx or dy or d:
-                        hello(part + self.hz[d], self.hs[d])
+        for dx, dy, d in FAR_FIRST:
+            part = 16 * self.X[dx] + 4 * self.Y[dy]
+            if dx or dy or d:
+                hello(part + self.hz[d], self.hs[d])
+            if d == 2:
                 hello(part + beyond, self.s)
         for o in (self.buddy, self.cross, self.diag):
             hello(self.me, o)
@@ -103,9 +102,9 @@
         d.wait_recv()
 
 
-def leg_one(pc, src, recv, sem_loc, ssem, rsem):
+def leg_one(pc, src, recv, sem_loc, ssem, rsem, columns=(0, 1)):
     for dx, dy, d in FAR_FIRST:
-        if not (dx or dy or d):
+        if not (dx or dy or d) or d // 2 not in columns:
             continue
         u = pc.U[d][dx]
 
@@ -117,9 +116,10 @@
                 device_id=(16 * pc.X[dx] + 4 * pc.Y[dy] + pc.hz[d], pc.hs[d]), device_id_type=MESH,
             ).start()
 
-    @pl.when(pc.relay)
-    def _():
-        pltpu.make_async_copy(tile_at(src, pc.row, 0), recv.at[pc.me], sem_loc).start()
+    if 0 in columns:
+        @pl.when(pc.relay)
+        def _():
+            pltpu.make_async_copy(tile_at(src, pc.row, 0), recv.at[pc.me], sem_loc).start()
 
 
 def leg_one_wait(pc, src, recv, sem_loc, ssem, rsem):
@@ -139,20 +139,24 @@
                 p = 16 * pc.X[dx] + 4 * pc.Y[dy] + pc.Z[e]
                 pltpu.make_async_remote_copy(
                     src_ref=send.at[p], dst_ref=tile_at(dst, pc.row, Q * pc.ds[e] + 128 * pc.dk[e]),
-                    send_sem=ssem, recv_sem=rsem, device_id=(p, pc.ds[e]), device_id_type=MESH,
+                    send_sem=ssem, recv_sem=rsem.at[pc.dk[e]], device_id=(p, pc.ds[e]), device_id_type=MESH,
                 ).start()
         pltpu.make_async_copy(send.at[pc.me], tile_at(dst, pc.row, Q * pc.s), sem_loc).start()
 
 
-def leg_two_wait(pc, recv, send, dst, sem_loc, ssem, rsem):
+def leg_two_wait(pc, recv, send, dst, sem_loc, ssem, rsem, column):
+    if column:
+        wait_tiles(recv, TILES // 2, ssem, rsem.at[1], pc, False)
+        return
+
     @pl.when(pc.relay)
     def _():
         pltpu.make_async_copy(send.at[pc.me], tile_at(dst, pc.row, Q * pc.s), sem_loc).wait()
-        wait_tiles(recv, TILES - 1, ssem, rsem, pc, False)
+        wait_tiles(recv, TILES // 2 - 1, ssem, rsem.at[0], pc, False)
 
     @pl.when(jnp.logical_not(pc.relay))
     def _():
-        wait_tiles(recv, TILES, ssem, rsem, pc, False)
+        wait_tiles(recv, TILES // 2, ssem, rsem.at[0], pc, False)
 
 
 def legs_sent(pc, recv, s1, s2, r1):
@@ -199,15 +203,16 @@
 
 
 def round_kernel(
-    src, tgt, rel_in, sidx_in, tidx_in, kidx_in, planrow_in, lim_in, plan_in,
-    o_src, o_tgt, o_rel,
-    rel, sidx, tidx, kidx, planrow, lim, plan,
+    src, tgt, rel_in, sidx_in, tidx_in, kidx_in, planrow_in, lim, plan_in, state_in,
+    o_new, o_tgt, o_rel,
+    rel, sidx, tidx, kidx, planrow, plan, state, o_src,
     raw, src_raw, low, table, heads, tails, kinds, query, head, tail, relrow, coef, gtail, ghead, grel, tg, sg,
     send1, recv1, send2, quarter, recv3, send4,
     t1, t2send, t2, half, halfin, halfx, rg, r1buf, r2buf, r2send, rax, invcol, inv,
     sem_in, sem_loc, s1, r1, s2, r2, s3, r3, s4, r4, sag, rag, sbk, rbk, st, rt, srel, rrel,
 ):
     pc = Place()
+    barrier = pc.greet()
     cin = []
     for k in range(2):
         g = lax.rem(pc.z + pc.zl + 3 * k - 2 * k * pc.zl, 4)
@@ -215,13 +220,12 @@
         cin.append(pltpu.make_async_copy(tgt.at[:, at], raw.at[:, pl.ds(128 * k, 128)], sem_in.at[3 + k]))
     small = [
         pltpu.make_async_copy(a, b, sem_in.at[5 + i]) for i, (a, b) in enumerate((
-            (rel_in, rel), (sidx_in, sidx), (tidx_in, tidx), (kidx_in, kidx), (planrow_in, planrow), (lim_in, lim), (plan_in, plan),
+            (rel_in, rel), (sidx_in, sidx), (tidx_in, tidx), (kidx_in, kidx), (planrow_in, planrow), (plan_in, plan), (state_in, state),
         ))
     ]
     csrc = pltpu.make_async_copy(src, src_raw, sem_in.at[1])
     for c in (*cin, *small, csrc):
         c.start()
-    barrier = pc.greet()
     for c in cin:
         c.wait()
     send1[...] = raw[...].astype(BF)
@@ -271,25 +275,31 @@
         return carry
 
     lax.fori_loop(0, EDGES // CHUNK, mark_tails, 0)
-    leg_two_wait(pc, recv1, send2, table, sem_loc.at[1], s2, r2)
-
     def cp(out, q, c, o, i, ss, rs):
-        ref = out.at[pl.ds(c * CHROWS, CHROWS), lanes(q)]
+        k, row, rows = PIECES[c]
+        ref = out.at[pl.ds(row, rows), pl.ds(pl.multiple_of(q * Q + 128 * k, 128), 128)]
         return pltpu.make_async_remote_copy(
             src_ref=ref, dst_ref=ref, send_sem=ss.at[i, c], recv_sem=rs.at[i, c],
             device_id=(pc.me, o), device_id_type=MESH,
         )
 
-    across = [cp(table, pc.s, c, pc.cross, 0, sag, rag) for c in range(CH)]
-    beside = [cp(table, pc.s, c, pc.buddy, 1, sag, rag) for c in range(CH)]
-    passed = [cp(table, pc.cross, c, pc.buddy, 2, sag, rag) for c in range(CH)]
-    for c in range(CH):
-        across[c].start()
-        beside[c].start()
+    def spread(out, ss, rs):
+        across = [cp(out, pc.s, c, pc.cross, 0, ss, rs) for c in range(CH)]
+        beside = [cp(out, pc.s, c, pc.buddy, 1, ss, rs) for c in range(CH)]
+        passed = [cp(out, pc.cross, c, pc.buddy, 2, ss, rs) for c in range(CH)]
+        return across, beside, passed
+
+    across, beside, passed = spread(table, sag, rag)
+    for k in range(2):
+        leg_two_wait(pc, recv1, send2, table, sem_loc.at[1], s2, r2, k)
+        for c in range(2 * k, 2 * k + 2):
+            across[c].start()
+            beside[c].start()
     for c in range(CH):
         beside[c].wait_recv()
     near = pl.ds(pl.multiple_of(pc.zl * 512, 512), 512)
     far = pl.ds(pl.multiple_of(512 - pc.zl * 512, 512), 512)
+
 
     def tails_near(c, carry):
         tail[:, chunk_at(c)] = dot(table[:, near], tails[near, chunk_at(c)]).astype(BF)
@@ -314,16 +324,14 @@
     def score_span(k, carry):
         base = pl.multiple_of(k * E_CH, 128)
         at = pl.ds(base, E_CH)
+        score = dot(query[:, at], tail[:, at], 0, 0)
         for b in range(E_CH // 128):
-            qb = query[:, pl.ds(pl.multiple_of(base + 128 * b, 128), 128)]
-            score = dot(qb, tail[:, at], 0, 0)
             for j in range(E_CH // 128):
-                u = score[:, 128 * j:128 * j + 128]
+                bend = jnp.tanh(0.5 * score[128 * b:128 * b + 128, 128 * j:128 * j + 128])
+                w = (0.5 * NEG_WEIGHT) * bend + 0.5 * NEG_WEIGHT
                 if j == b:
                     one = lax.broadcasted_iota(jnp.int32, (128, 128), 0) == lax.broadcasted_iota(jnp.int32, (128, 128), 1)
-                    w = jax.nn.sigmoid(jnp.where(one, -u, u)) * jnp.where(one, -1.0, NEG_WEIGHT)
-                else:
-                    w = jax.nn.sigmoid(u) * NEG_WEIGHT
+                    w = jnp.where(one, 0.5 * bend - 0.5, w)
                 coef[k, pl.ds(128 * b, 128), pl.ds(128 * j, 128)] = w.astype(BF)
         gtail[:, at] = dot(query[:, at], coef[k]).astype(BF)
         return carry
@@ -345,14 +353,15 @@
 
     ta = rc(tg.at[:, lanes(pc.diag)], t1.at[1], 0, pc.buddy)
     tb = rc(tg.at[:, lanes(pc.buddy)], t1.at[0], 1, pc.buddy)
-    tc = rc(t2send, t2, 5, pc.cross)
+    tc = [rc(t2send.at[:, pl.ds(128 * k, 128)], t2.at[:, pl.ds(128 * k, 128)], 5 + 9 * k, pc.cross) for k in range(2)]
     target_sum(far)
     ta.start()
     target_sum(near)
     tb.start()
     ta.wait_recv()
     t2send[...] = (tg[:, lanes(pc.cross)].astype(F32) + t1[1].astype(F32)).astype(BF)
-    tc.start()
+    tc[1].start()
+    tc[0].start()
     def query_span(k, carry):
         at = pl.ds(pl.multiple_of(k * E_CH, 128), E_CH)
         gq = dot(tail[:, at], coef[k], 1, 1)
@@ -373,29 +382,32 @@
     sa = rc(sg.at[:, lanes(pc.buddy)], halfin.at[0], 2, pc.buddy)
     sb = rc(sg.at[:, lanes(pc.diag)], halfin.at[1], 3, pc.buddy)
     ra = rc(rg, r1buf, 4, pc.buddy)
+    def quarter_column(k):
+        tc[k].wait_recv()
+        at = pl.ds(pl.multiple_of(pc.s * Q + 128 * k, 128), 128)
+        col = pl.ds(128 * k, 128)
+        quarter[:, col] = (tg[:, at].astype(F32) + t1[0, :, col].astype(F32) + t2[:, col].astype(F32)).astype(BF)
+        leg_one(pc, quarter, recv3, sem_loc.at[2], s3, r3, (k,))
+
+    sc = rc(half.at[0], halfx.at[1], 7, pc.cross)
+    sd = rc(half.at[1], halfx.at[0], 8, pc.cross)
+    source_sum(near)
+    sa.start()
+    tb.wait_recv()
+    quarter_column(1)
     rg[:, 0:D] = dot(kinds[...], grel[...], 1, 1)
     rg[:, D:512] = jnp.zeros((REL, 512 - D), F32)
     ra.start()
-    source_sum(near)
-    sa.start()
-    tb.wait_recv()
-    tc.wait_recv()
-    quarter[...] = (tg[:, lanes(pc.s)].astype(F32) + t1[0].astype(F32) + t2[...].astype(F32)).astype(BF)
-    leg_one(pc, quarter, recv3, sem_loc.at[2], s3, r3)
-
+    quarter_column(0)
     ra.wait_recv()
     r2send[...] = rg[...] + r1buf[...]
     rb = rc(r2send, r2buf, 6, pc.cross)
     rb.start()
-    sc = rc(half.at[0], halfx.at[1], 7, pc.cross)
-    sd = rc(half.at[1], halfx.at[0], 8, pc.cross)
     sa.wait_recv()
     half[0] = (sg[:, lanes(pc.s)].astype(F32) + halfin[0].astype(F32)).astype(BF)
     sc.start()
     source_sum(far)
     sb.start()
-    sb.wait_recv()
-    half[1] = (sg[:, lanes(pc.cross)].astype(F32) + halfin[1].astype(F32)).astype(BF)
 
     col = pl.ds(pl.multiple_of(pc.s * 128, 128), 128)
     px = [16 * x + 4 * pc.y + pc.z for x in pc.X[1:]]
@@ -416,44 +428,55 @@
         d.wait_recv()
         return (rax[i, 0] + rax[i, 1]) + (rax[i, 2] + rax[i, 3])
 
+    sb.wait_recv()
+    half[1] = (sg[:, lanes(pc.cross)].astype(F32) + halfin[1].astype(F32)).astype(BF)
+    sd.start()
     rb.wait_recv()
     axis(0, pc.x, px, r2send[:, col] + r2buf[:, col])
     leg_one_wait(pc, quarter, recv3, sem_loc.at[2], s3, r3)
     leg_two(pc, recv3, lambda i: inv[i, 0], send4, o_tgt, sem_loc.at[3], s4, r4)
-    sd.start()
     axis(1, pc.y, py, axis_wait(0))
     axis(2, pc.z, pz, axis_wait(1))
-
-    leg_two_wait(pc, recv3, send4, o_tgt, sem_loc.at[3], s4, r4)
-    across2 = [cp(o_tgt, pc.s, c, pc.cross, 0, sbk, rbk) for c in range(CH)]
-    beside2 = [cp(o_tgt, pc.s, c, pc.buddy, 1, sbk, rbk) for c in range(CH)]
-    passed2 = [cp(o_tgt, pc.cross, c, pc.buddy, 2, sbk, rbk) for c in range(CH)]
-    for c in range(CH):
-        across2[c].start()
-        beside2[c].start()
-
+    across2, beside2, passed2 = spread(o_tgt, sbk, rbk)
+    for k in range(2):
+        leg_two_wait(pc, recv3, send4, o_tgt, sem_loc.at[3], s4, r4, k)
+        for c in range(2 * k, 2 * k + 2):
+            across2[c].start()
+            beside2[c].start()
     sc.wait_recv()
     sd.wait_recv()
+    def source_step(q):
+        at = lanes(q)
+        grad = o_src[:, at].astype(F32)
+        total = state[:, at] + jnp.sum(grad * grad, axis=0, keepdims=True) * (1.0 / D)
+        o_new[:, at] = src_raw[:, at] - grad * (LEARN_RATE / jnp.sqrt(total))
+
     o_src[:, lanes(pc.s)] = (half[0].astype(F32) + halfx[0].astype(F32)).astype(BF)
     o_src[:, lanes(pc.cross)] = (half[1].astype(F32) + halfx[1].astype(F32)).astype(BF)
     se = rc(o_src.at[:, lanes(pc.s)], o_src.at[:, lanes(pc.s)], 9, pc.buddy)
     sf = rc(o_src.at[:, lanes(pc.cross)], o_src.at[:, lanes(pc.cross)], 10, pc.buddy)
     se.start()
     sf.start()
-    for c in range(CH):
-        across2[c].wait_recv()
-        passed2[c].start()
     o_rel[:, col] = axis_wait(2)
     rel_out = [rc(o_rel.at[:, col], o_rel.at[:, col], 11 + i, o) for i, o in enumerate((pc.buddy, pc.cross, pc.diag))]
     for c in rel_out:
         c.start()
+    source_step(pc.s)
+    source_step(pc.cross)
+    for c in range(CH):
+        across2[c].wait_recv()
+        passed2[c].start()
+    se.wait_recv()
+    sf.wait_recv()
+    source_step(pc.buddy)
+    source_step(pc.diag)
     for c in range(CH):
         beside2[c].wait_recv()
         passed2[c].wait_recv()
-    for c in (se, sf, *rel_out):
+    for c in rel_out:
         c.wait_recv()
 
-    for c in (ta, tb, tc, sa, sb, sc, sd, se, sf, ra, rb, *rel_out, *across, *beside, *passed, *across2, *beside2, *passed2):
+    for c in (ta, tb, *tc, sa, sb, sc, sd, se, sf, ra, rb, *rel_out, *across, *beside, *passed, *across2, *beside2, *passed2):
         c.wait_send()
     for i in range(3):
         axis_wait(i, True)
@@ -461,7 +484,7 @@
     legs_sent(pc, recv3, s3, s4, r3)
 
 
-def training_round(source_t, target_t, relation, sidx, tidx, kidx, counts, plan):
+def training_round(source_t, target_t, relation, sidx, tidx, kidx, counts, plan, state):
     vm = pl.BlockSpec(memory_space=pltpu.VMEM)
     hb = pl.BlockSpec(memory_space=pltpu.HBM)
     dma = pltpu.SemaphoreType.DMA
@@ -477,17 +500,17 @@
 
     tiles = bf(64, 16, 128)
     kept = [
-        pltpu.with_memory_space_constraint(a, pltpu.HBM) for a in (source_t, target_t, relation, sidx, tidx, kidx, plan[None, :])
+        pltpu.with_memory_space_constraint(a, pltpu.HBM) for a in (source_t, target_t, relation, sidx, tidx, kidx, plan[None, :], plan, state)
     ]
     return pl.pallas_call(
         round_kernel,
         out_shape=(
-            jax.ShapeDtypeStruct((D, ROWS), BF), jax.ShapeDtypeStruct((D, ROWS), BF), jax.ShapeDtypeStruct((REL, 512), F32),
+            jax.ShapeDtypeStruct((D, ROWS), F32), jax.ShapeDtypeStruct((D, ROWS), BF), jax.ShapeDtypeStruct((REL, 512), F32),
         ),
-        in_specs=[hb] * 9,
+        in_specs=[hb] * 7 + [pl.BlockSpec(memory_space=pltpu.SMEM)] + [hb] * 2,
         out_specs=(vm, vm, vm),
         scratch_shapes=[
-            f(REL, D), i32(1, EDGES), i32(1, EDGES), i32(1, EDGES), i32(1, 64), pltpu.SMEM((1,), jnp.int32), pltpu.SMEM((64,), jnp.int32),
+            f(REL, D), i32(1, EDGES), i32(1, EDGES), i32(1, EDGES), i32(1, 64), pltpu.SMEM((64,), jnp.int32), f(1, ROWS), bf(D, ROWS),
             f(D, Q), f(D, ROWS), bf(D, ROWS), bf(D, ROWS), bf(ROWS, EDGES), bf(ROWS, EDGES), bf(REL, EDGES),
             bf(D, EDGES), bf(D, EDGES), bf(D, EDGES), f(D, EDGES), bf(SPANS, E_CH, E_CH),
             bf(D, EDGES), bf(D, EDGES), bf(D, EDGES), bf(D, ROWS), bf(D, ROWS),
@@ -495,34 +518,31 @@
             bf(2, D, Q), bf(D, Q), bf(D, Q), bf(2, D, Q), bf(2, D, Q), bf(2, D, Q),
             f(REL, 512), f(REL, 512), f(REL, 512), f(REL, 512), f(3, 4, REL, 128),
             pltpu.VMEM((64, 128), jnp.int32), pltpu.SMEM((64, 128), jnp.int32),
-            dma((12,)), dma((4,)), dma, dma, dma, dma, dma, dma, dma, dma,
-            dma((3, CH)), dma((3, CH)), dma((3, CH)), dma((3, CH)), dma((14,)), dma((14,)), dma((3,)), dma((3,)),
+            dma((13,)), dma((4,)), dma, dma, dma, dma((2,)), dma, dma, dma, dma((2,)),
+            dma((3, CH)), dma((3, CH)), dma((3, CH)), dma((3, CH)), dma((15,)), dma((15,)), dma((3,)), dma((3,)),
         ],
         compiler_params=pltpu.CompilerParams(collective_id=0, has_side_effects=True, vmem_limit_bytes=46 << 20),
         name="training_round",
-    )(*kept, counts, pltpu.with_memory_space_constraint(plan, pltpu.HBM))
-
-
-def adagrad_kernel(ws, ss, gs, wt, st, gt, wr, sr, gr, o_s, o_t, o_r, buf, sem):
-    copies = []
+    )(*kept[:7], counts, *kept[7:])
+
+
+def adagrad_kernel(new, wt, st, gt, wr, sr, gr, o_s, o_t, o_r, buf, sem):
+    copies = [pltpu.make_async_copy(new, o_s, sem.at[ROWS // Q])]
+    copies[0].start()
     z = lax.rem(lax.axis_index("bucket"), 4)
-    for i, (w, s, g, o) in enumerate(((ws, ss, gs, o_s), (wt, st, gt, o_t))):
-        for q in range(ROWS // Q):
-            at = pl.ds(q * Q, Q)
-            if i == 0:
-                grad = g[:, at].astype(F32)
-            else:
-                cols = [pl.multiple_of(128 * group_column(q // 2, 2 * (q % 2) + h, z), 128) for h in range(2)]
-                grad = jnp.concatenate([g[:, pl.ds(c, 128)] for c in cols], axis=1).astype(F32)
-            total = s[:, at] + jnp.sum(grad * grad, axis=0, keepdims=True) * (1.0 / D)
-            buf[i, q] = w[:, at] - (LEARN_RATE * grad) / jnp.sqrt(total)
-            copies.append(pltpu.make_async_copy(buf.at[i, q], o.at[:, at], sem.at[i, q]))
-            copies[-1].start()
+    for q in range(ROWS // Q):
+        at = pl.ds(q * Q, Q)
+        cols = [pl.multiple_of(128 * group_column(q // 2, 2 * (q % 2) + h, z), 128) for h in range(2)]
+        grad = jnp.concatenate([gt[:, pl.ds(c, 128)] for c in cols], axis=1).astype(F32)
+        total = st[:, at] + jnp.sum(grad * grad, axis=0, keepdims=True) * (1.0 / D)
+        buf[q] = wt[:, at] - grad * (LEARN_RATE / jnp.sqrt(total))
+        copies.append(pltpu.make_async_copy(buf.at[q], o_t.at[:, at], sem.at[q]))
+        copies[-1].start()
     grad = gr[:, 0:D]
     same = lax.broadcasted_iota(jnp.int32, (REL, REL), 0) == lax.broadcasted_iota(jnp.int32, (REL, REL), 1)
     state = jnp.sum(jnp.where(same, sr[...], 0.0), axis=1, keepdims=True)
     total = state + jnp.sum(grad * grad, axis=1, keepdims=True) * (1.0 / D)
-    o_r[...] = wr[...] - (LEARN_RATE * grad) / jnp.sqrt(total)
+    o_r[...] = wr[...] - grad * (LEARN_RATE / jnp.sqrt(total))
     for c in copies:
         c.wait()
 
@@ -535,9 +555,9 @@
         out_shape=(
             jax.ShapeDtypeStruct((D, ROWS), F32), jax.ShapeDtypeStruct((D, ROWS), F32), jax.ShapeDtypeStruct((REL, D), F32),
         ),
-        in_specs=[vm] * 9,
+        in_specs=[vm] * 7,
         out_specs=(hb, hb, vm),
-        scratch_shapes=[pltpu.VMEM((2, ROWS // Q, D, Q), F32), pltpu.SemaphoreType.DMA((2, ROWS // Q))],
+        scratch_shapes=[pltpu.VMEM((ROWS // Q, D, Q), F32), pltpu.SemaphoreType.DMA((ROWS // Q + 1,))],
         compiler_params=pltpu.CompilerParams(vmem_limit_bytes=24 << 20),
         name="adagrad",
     )(*args)
@@ -546,12 +566,10 @@
 def per_device(source_table, target_table, source_state, target_state, relation, relation_state,
                plan, source_index, target_index, relation_index, edge_counts):
     source_t, target_t = source_table.T, target_table.T
-    sg, tg, rg = training_round(
-        source_t, target_t, relation, source_index, target_index, relation_index, edge_counts, plan
+    new, tg, rg = training_round(
+        source_t, target_t, relation, source_index, target_index, relation_index, edge_counts, plan, source_state[None, :]
     )
-    ns, nt, nr = adagrad(
-        source_t, source_state[None, :], sg, target_t, target_state[None, :], tg, relation, relation_state[None, :], rg
-    )
+    ns, nt, nr = adagrad(new, target_t, target_state[None, :], tg, relation, relation_state[None, :], rg)
     return ns.T, nt.T, nr
 
 

time: 82 us -> 77.6 us (0.946)
  Pallas kernels: 80.5 us -> 76.1 us
    pallas_call x1, Pallas kernels: 77.3 us -> 73.8 us  [training_round(): pl.pallas_call(round_kernel, out_shape=(jax.ShapeDtypeStruct((D, ROWS), F...]
where the time goes in v4:
time: 77.6 us; the launch traced here: 77.5 us
  Pallas kernels  76.1 us (98%)
  between operations  1.35 us (2%)
    pallas_call x1, Pallas kernels, training_round(): pl.pallas_call(round_kernel, out_shape=(jax.ShapeDtypeStruct((D, ROWS), F...  73.8 us
    pallas_call x1, Pallas kernels, adagrad(): pl.pallas_call(adagrad_kernel, out_shape=(jax.ShapeDtypeStruct((D, ROWS),...  2.36 us

profile of v4, /device:TPU:1, one launch (start us, length us, event | category | flops | bytes accessed | tf_op | source)
XLA Modules:
  0.0 77.5 jit_solution(335883173759444538)
XLA Ops:
  1.3 0.0 copy-start
  1.3 0.0 copy-start.1
  1.3 0.0 copy-start.2
  1.3 0.0 copy-start.3
  1.3 73.8 %training_round.1 = (f32[400,1024]{1,0:T(8,128)S(1)}, bf16[400,1024]{1,0:T(8,128)(2,1)S(1)}, f32[16,512]{1,0:T(8,128)S(1)}) custom-call(f32[400,1024]{1,0:T(8,128)} %bitcast.12, f32[400,1024]{1,0:T(8,128)} %bitcast.8, f32[16,400]{1,0:T(8,128)} %wr.1, s32[1,2560]{1,0:T(1,128)} %sidx_in.1, s32[1,2560]{1,0:T(1,128)} %tidx_in.1, s32[1,2560]{1,0:T(1,128)} %kidx_in.1, ...), custom_call_target="tpu_custom_call" | custom-call | tf_op jit(solution)/shard_map/training_round/pallas_call | solution.py:505
  75.1 0.0 copy-done
  75.1 0.0 copy-done.1
  75.1 0.0 copy-done.2
  75.1 0.0 copy-done.3
  75.2 2.4 %adagrad.1 = (f32[400,1024]{1,0:T(8,128)}, f32[400,1024]{1,0:T(8,128)}, f32[16,400]{1,0:T(8,128)}) custom-call(f32[400,1024]{1,0:T(8,128)S(1)} %get-tuple-element.9.new, f32[400,1024]{1,0:T(8,128)S(1)} %bitcast.9, f32[1,1024]{1,0:T(1,128)S(1)} %bitcast.10, bf16[400,1024]{1,0:T(8,128)(2,1)S(1)} %get-tuple-element.10.gt, f32[16,400]{1,0:T(8,128)S(1)} %copy-done.1, ...), custom_call_target="tpu_custom_call" | custom-call | tf_op jit(solution)/shard_map/adagrad/pallas_call | solution.py:553
Async XLA Ops:
  1.3 73.8 %copy-start = (f32[1024,400]{0,1:T(8,128)S(1)}, f32[1024,400]{0,1:T(8,128)}, u32[]{:S(2)}) copy-start(f32[1024,400]{0,1:T(8,128)} %param.12) | copy-start | bytes 4915204
  1.3 73.8 %copy-start.1 = (f32[16,400]{1,0:T(8,128)S(1)}, f32[16,400]{1,0:T(8,128)}, u32[]{:S(2)}) copy-start(f32[16,400]{1,0:T(8,128)} %wr.1) | copy-start | bytes 76804
  1.3 73.8 %copy-start.2 = (f32[1024]{0:T(1024)S(1)}, f32[1024]{0:T(1024)}, u32[]{:S(2)}) copy-start(f32[1024]{0:T(1024)} %param.14) | copy-start | bytes 12292
  1.3 73.8 %copy-start.3 = (f32[16]{0:T(128)S(1)}, f32[16]{0:T(128)}, u32[]{:S(2)}) copy-start(f32[16]{0:T(128)} %param.16) | copy-start | bytes 196

commit v5 on v4

--- a/solution.py
+++ b/solution.py
@@ -212,7 +212,6 @@
     sem_in, sem_loc, s1, r1, s2, r2, s3, r3, s4, r4, sag, rag, sbk, rbk, st, rt, srel, rrel,
 ):
     pc = Place()
-    barrier = pc.greet()
     cin = []
     for k in range(2):
         g = lax.rem(pc.z + pc.zl + 3 * k - 2 * k * pc.zl, 4)
@@ -224,7 +223,10 @@
         ))
     ]
     csrc = pltpu.make_async_copy(src, src_raw, sem_in.at[1])
-    for c in (*cin, *small, csrc):
+    for c in (*cin, csrc):
+        c.start()
+    barrier = pc.greet()
+    for c in small:
         c.start()
     for c in cin:
         c.wait()
@@ -324,10 +326,10 @@
     def score_span(k, carry):
         base = pl.multiple_of(k * E_CH, 128)
         at = pl.ds(base, E_CH)
-        score = dot(query[:, at], tail[:, at], 0, 0)
         for b in range(E_CH // 128):
+            score = dot(query[:, pl.ds(pl.multiple_of(base + 128 * b, 128), 128)], tail[:, at], 0, 0)
             for j in range(E_CH // 128):
-                bend = jnp.tanh(0.5 * score[128 * b:128 * b + 128, 128 * j:128 * j + 128])
+                bend = jnp.tanh(0.5 * score[:, 128 * j:128 * j + 128])
                 w = (0.5 * NEG_WEIGHT) * bend + 0.5 * NEG_WEIGHT
                 if j == b:
                     one = lax.broadcasted_iota(jnp.int32, (128, 128), 0) == lax.broadcasted_iota(jnp.int32, (128, 128), 1)
@@ -374,14 +376,6 @@
         grel[:, at] = jnp.concatenate([gr * hr + gm * hm, gm * hr - gr * hm], axis=0).astype(BF)
         return carry
 
-    lax.fori_loop(0, SPANS, query_span, 0)
-
-    def source_sum(part):
-        sg[:, part] = dot(ghead[...], heads[part, :], 1, 1).astype(BF)
-
-    sa = rc(sg.at[:, lanes(pc.buddy)], halfin.at[0], 2, pc.buddy)
-    sb = rc(sg.at[:, lanes(pc.diag)], halfin.at[1], 3, pc.buddy)
-    ra = rc(rg, r1buf, 4, pc.buddy)
     def quarter_column(k):
         tc[k].wait_recv()
         at = pl.ds(pl.multiple_of(pc.s * Q + 128 * k, 128), 128)
@@ -389,8 +383,17 @@
         quarter[:, col] = (tg[:, at].astype(F32) + t1[0, :, col].astype(F32) + t2[:, col].astype(F32)).astype(BF)
         leg_one(pc, quarter, recv3, sem_loc.at[2], s3, r3, (k,))
 
+    lax.fori_loop(0, SPANS, query_span, 0)
+
+    def source_sum(part):
+        sg[:, part] = dot(ghead[...], heads[part, :], 1, 1).astype(BF)
+
+    sa = rc(sg.at[:, lanes(pc.buddy)], halfin.at[0], 2, pc.buddy)
+    sb = rc(sg.at[:, lanes(pc.diag)], halfin.at[1], 3, pc.buddy)
+    ra = rc(rg, r1buf, 4, pc.buddy)
+    rb = rc(r2send, r2buf, 6, pc.cross)
     sc = rc(half.at[0], halfx.at[1], 7, pc.cross)
-    sd = rc(half.at[1], halfx.at[0], 8, pc.cross)
+    sd = [rc(half.at[1, pl.ds(a, n)], halfx.at[0, pl.ds(a, n)], i, pc.cross) for i, a, n in ((8, 0, 208), (15, 208, 192))]
     source_sum(near)
     sa.start()
     tb.wait_recv()
@@ -401,7 +404,6 @@
     quarter_column(0)
     ra.wait_recv()
     r2send[...] = rg[...] + r1buf[...]
-    rb = rc(r2send, r2buf, 6, pc.cross)
     rb.start()
     sa.wait_recv()
     half[0] = (sg[:, lanes(pc.s)].astype(F32) + halfin[0].astype(F32)).astype(BF)
@@ -430,11 +432,12 @@
 
     sb.wait_recv()
     half[1] = (sg[:, lanes(pc.cross)].astype(F32) + halfin[1].astype(F32)).astype(BF)
-    sd.start()
+    sd[0].start()
     rb.wait_recv()
     axis(0, pc.x, px, r2send[:, col] + r2buf[:, col])
     leg_one_wait(pc, quarter, recv3, sem_loc.at[2], s3, r3)
     leg_two(pc, recv3, lambda i: inv[i, 0], send4, o_tgt, sem_loc.at[3], s4, r4)
+    sd[1].start()
     axis(1, pc.y, py, axis_wait(0))
     axis(2, pc.z, pz, axis_wait(1))
     across2, beside2, passed2 = spread(o_tgt, sbk, rbk)
@@ -444,7 +447,8 @@
             across2[c].start()
             beside2[c].start()
     sc.wait_recv()
-    sd.wait_recv()
+    sd[0].wait_recv()
+    sd[1].wait_recv()
     def source_step(q):
         at = lanes(q)
         grad = o_src[:, at].astype(F32)
@@ -457,13 +461,14 @@
     sf = rc(o_src.at[:, lanes(pc.cross)], o_src.at[:, lanes(pc.cross)], 10, pc.buddy)
     se.start()
     sf.start()
-    o_rel[:, col] = axis_wait(2)
-    rel_out = [rc(o_rel.at[:, col], o_rel.at[:, col], 11 + i, o) for i, o in enumerate((pc.buddy, pc.cross, pc.diag))]
-    for c in rel_out:
-        c.start()
     source_step(pc.s)
     source_step(pc.cross)
     for c in range(CH):
+        if c == CH // 2:
+            o_rel[:, col] = axis_wait(2)
+            rel_out = [rc(o_rel.at[:, col], o_rel.at[:, col], 11 + i, o) for i, o in enumerate((pc.buddy, pc.cross, pc.diag))]
+            for r in rel_out:
+                r.start()
         across2[c].wait_recv()
         passed2[c].start()
     se.wait_recv()
@@ -476,7 +481,7 @@
     for c in rel_out:
         c.wait_recv()
 
-    for c in (ta, tb, *tc, sa, sb, sc, sd, se, sf, ra, rb, *rel_out, *across, *beside, *passed, *across2, *beside2, *passed2):
+    for c in (ta, tb, *tc, sa, sb, sc, *sd, se, sf, ra, rb, *rel_out, *across, *beside, *passed, *across2, *beside2, *passed2):
         c.wait_send()
     for i in range(3):
         axis_wait(i, True)
@@ -519,7 +524,7 @@
             f(REL, 512), f(REL, 512), f(REL, 512), f(REL, 512), f(3, 4, REL, 128),
             pltpu.VMEM((64, 128), jnp.int32), pltpu.SMEM((64, 128), jnp.int32),
             dma((13,)), dma((4,)), dma, dma, dma, dma((2,)), dma, dma, dma, dma((2,)),
-            dma((3, CH)), dma((3, CH)), dma((3, CH)), dma((3, CH)), dma((15,)), dma((15,)), dma((3,)), dma((3,)),
+            dma((3, CH)), dma((3, CH)), dma((3, CH)), dma((3, CH)), dma((16,)), dma((16,)), dma((3,)), dma((3,)),
         ],
         compiler_params=pltpu.CompilerParams(collective_id=0, has_side_effects=True, vmem_limit_bytes=46 << 20),
         name="training_round",
@@ -527,8 +532,11 @@
 
 
 def adagrad_kernel(new, wt, st, gt, wr, sr, gr, o_s, o_t, o_r, buf, sem):
-    copies = [pltpu.make_async_copy(new, o_s, sem.at[ROWS // Q])]
-    copies[0].start()
+    copies = []
+    for q in range(ROWS // Q):
+        at = pl.ds(q * 96 if q else 0, 96 if q < 3 else 112)
+        copies.append(pltpu.make_async_copy(new.at[at, :], o_s.at[at, :], sem.at[ROWS // Q + q]))
+        copies[-1].start()
     z = lax.rem(lax.axis_index("bucket"), 4)
     for q in range(ROWS // Q):
         at = pl.ds(q * Q, Q)
@@ -557,7 +565,7 @@
         ),
         in_specs=[vm] * 7,
         out_specs=(hb, hb, vm),
-        scratch_shapes=[pltpu.VMEM((ROWS // Q, D, Q), F32), pltpu.SemaphoreType.DMA((ROWS // Q + 1,))],
+        scratch_shapes=[pltpu.VMEM((ROWS // Q, D, Q), F32), pltpu.SemaphoreType.DMA((2 * ROWS // Q,))],
         compiler_params=pltpu.CompilerParams(vmem_limit_bytes=24 << 20),
         name="adagrad",
     )(*args)

time: 77.6 us -> 77.3 us (level)
  no operation moved by 1% of the time
where the time goes in v5:
time: 77.3 us; the launch traced here: 77.2 us
  Pallas kernels  75.9 us (98%)
  between operations  1.35 us (2%)
    pallas_call x1, Pallas kernels, training_round(): pl.pallas_call(round_kernel, out_shape=(jax.ShapeDtypeStruct((D, ROWS), F...  73.5 us
    pallas_call x1, Pallas kernels, adagrad(): pl.pallas_call(adagrad_kernel, out_shape=(jax.ShapeDtypeStruct((D, ROWS),...  2.38 us

profile of v5, /device:TPU:1, one launch (start us, length us, event | category | flops | bytes accessed | tf_op | source)
XLA Modules:
  0.0 77.2 jit_solution(1381692253897425138)
XLA Ops:
  1.3 0.0 copy-start
  1.3 0.0 copy-start.1
  1.3 0.0 copy-start.2
  1.3 0.0 copy-start.3
  1.3 73.5 %training_round.1 = (f32[400,1024]{1,0:T(8,128)S(1)}, bf16[400,1024]{1,0:T(8,128)(2,1)S(1)}, f32[16,512]{1,0:T(8,128)S(1)}) custom-call(f32[400,1024]{1,0:T(8,128)} %bitcast.12, f32[400,1024]{1,0:T(8,128)} %bitcast.8, f32[16,400]{1,0:T(8,128)} %wr.1, s32[1,2560]{1,0:T(1,128)} %sidx_in.1, s32[1,2560]{1,0:T(1,128)} %tidx_in.1, s32[1,2560]{1,0:T(1,128)} %kidx_in.1, ...), custom_call_target="tpu_custom_call" | custom-call | tf_op jit(solution)/shard_map/training_round/pallas_call | solution.py:510
  74.8 0.0 copy-done
  74.8 0.0 copy-done.1
  74.8 0.0 copy-done.2
  74.8 0.0 copy-done.3
  74.9 2.4 %adagrad.1 = (f32[400,1024]{1,0:T(8,128)}, f32[400,1024]{1,0:T(8,128)}, f32[16,400]{1,0:T(8,128)}) custom-call(f32[400,1024]{1,0:T(8,128)S(1)} %get-tuple-element.9.new, f32[400,1024]{1,0:T(8,128)S(1)} %bitcast.9, f32[1,1024]{1,0:T(1,128)S(1)} %bitcast.10, bf16[400,1024]{1,0:T(8,128)(2,1)S(1)} %get-tuple-element.10.gt, f32[16,400]{1,0:T(8,128)S(1)} %copy-done.1, ...), custom_call_target="tpu_custom_call" | custom-call | tf_op jit(solution)/shard_map/adagrad/pallas_call | solution.py:561
Async XLA Ops:
  1.3 73.5 %copy-start = (f32[1024,400]{0,1:T(8,128)S(1)}, f32[1024,400]{0,1:T(8,128)}, u32[]{:S(2)}) copy-start(f32[1024,400]{0,1:T(8,128)} %param.12) | copy-start | bytes 4915204
  1.3 73.5 %copy-start.1 = (f32[16,400]{1,0:T(8,128)S(1)}, f32[16,400]{1,0:T(8,128)}, u32[]{:S(2)}) copy-start(f32[16,400]{1,0:T(8,128)} %wr.1) | copy-start | bytes 76804
  1.3 73.5 %copy-start.2 = (f32[1024]{0:T(1024)S(1)}, f32[1024]{0:T(1024)}, u32[]{:S(2)}) copy-start(f32[1024]{0:T(1024)} %param.14) | copy-start | bytes 12292
  1.3 73.5 %copy-start.3 = (f32[16]{0:T(128)S(1)}, f32[16]{0:T(128)}, u32[]{:S(2)}) copy-start(f32[16]{0:T(128)} %param.16) | copy-start | bytes 196

commit v6 on v5

--- a/solution.py
+++ b/solution.py
@@ -338,7 +338,8 @@
         gtail[:, at] = dot(query[:, at], coef[k]).astype(BF)
         return carry
 
-    lax.fori_loop(0, SPANS, score_span, 0)
+    for k in range(SPANS):
+        score_span(k, 0)
 
     def rc(src_ref, dst_ref, i, o):
         return pltpu.make_async_remote_copy(
@@ -383,7 +384,8 @@
         quarter[:, col] = (tg[:, at].astype(F32) + t1[0, :, col].astype(F32) + t2[:, col].astype(F32)).astype(BF)
         leg_one(pc, quarter, recv3, sem_loc.at[2], s3, r3, (k,))
 
-    lax.fori_loop(0, SPANS, query_span, 0)
+    for k in range(SPANS):
+        query_span(k, 0)
 
     def source_sum(part):
         sg[:, part] = dot(ghead[...], heads[part, :], 1, 1).astype(BF)

time: 77.3 us -> 77.7 us (level)
  no operation moved by 1% of the time
where the time goes in v6:
time: 77.7 us; the launch traced here: 77.6 us
  Pallas kernels  76.1 us (98%)
  between operations  1.53 us (2%)
    pallas_call x1, Pallas kernels, training_round(): pl.pallas_call(round_kernel, out_shape=(jax.ShapeDtypeStruct((D, ROWS), F...  73.7 us
    pallas_call x1, Pallas kernels, adagrad(): pl.pallas_call(adagrad_kernel, out_shape=(jax.ShapeDtypeStruct((D, ROWS),...  2.38 us

profile of v6, /device:TPU:1, one launch (start us, length us, event | category | flops | bytes accessed | tf_op | source)
XLA Modules:
  0.0 77.6 jit_solution(1634816173743376095)
XLA Ops:
  1.3 0.0 copy-start
  1.3 0.0 copy-start.1
  1.3 0.0 copy-start.2
  1.3 0.0 copy-start.3
  1.3 73.7 %training_round.1 = (f32[400,1024]{1,0:T(8,128)S(1)}, bf16[400,1024]{1,0:T(8,128)(2,1)S(1)}, f32[16,512]{1,0:T(8,128)S(1)}) custom-call(f32[400,1024]{1,0:T(8,128)} %bitcast.12, f32[400,1024]{1,0:T(8,128)} %bitcast.8, f32[16,400]{1,0:T(8,128)} %wr.1, s32[1,2560]{1,0:T(1,128)} %sidx_in.1, s32[1,2560]{1,0:T(1,128)} %tidx_in.1, s32[1,2560]{1,0:T(1,128)} %kidx_in.1, ...), custom_call_target="tpu_custom_call" | custom-call | tf_op jit(solution)/shard_map/training_round/pallas_call | solution.py:512
  75.0 0.0 copy-done
  75.0 0.0 copy-done.1
  75.0 0.0 copy-done.2
  75.1 0.0 copy-done.3
  75.1 2.4 %adagrad.1 = (f32[400,1024]{1,0:T(8,128)}, f32[400,1024]{1,0:T(8,128)}, f32[16,400]{1,0:T(8,128)}) custom-call(f32[400,1024]{1,0:T(8,128)S(1)} %get-tuple-element.9.new, f32[400,1024]{1,0:T(8,128)S(1)} %bitcast.9, f32[1,1024]{1,0:T(1,128)S(1)} %bitcast.10, bf16[400,1024]{1,0:T(8,128)(2,1)S(1)} %get-tuple-element.10.gt, f32[16,400]{1,0:T(8,128)S(1)} %copy-done.1, ...), custom_call_target="tpu_custom_call" | custom-call | tf_op jit(solution)/shard_map/adagrad/pallas_call | solution.py:563
Async XLA Ops:
  1.3 73.7 %copy-start = (f32[1024,400]{0,1:T(8,128)S(1)}, f32[1024,400]{0,1:T(8,128)}, u32[]{:S(2)}) copy-start(f32[1024,400]{0,1:T(8,128)} %param.12) | copy-start | bytes 4915204
  1.3 73.7 %copy-start.1 = (f32[16,400]{1,0:T(8,128)S(1)}, f32[16,400]{1,0:T(8,128)}, u32[]{:S(2)}) copy-start(f32[16,400]{1,0:T(8,128)} %wr.1) | copy-start | bytes 76804
  1.3 73.7 %copy-start.2 = (f32[1024]{0:T(1024)S(1)}, f32[1024]{0:T(1024)}, u32[]{:S(2)}) copy-start(f32[1024]{0:T(1024)} %param.14) | copy-start | bytes 12292
  1.3 73.7 %copy-start.3 = (f32[16]{0:T(128)S(1)}, f32[16]{0:T(128)}, u32[]{:S(2)}) copy-start(f32[16]{0:T(128)} %param.16) | copy-start | bytes 196
